TPU v7x, 32 devices: a whole 2x2x4 slice. The times are simulated.
32 devices in a mesh: grp: 2 (over x), row: 8 (over z, y), col: 2 (over core).
Axes of the slice: x: 2, y: 2, z: 4, core: 2. Of those that a mesh axis runs over, the one named last changes fastest.
Arguments:
- order_field: float32 [4, 16, 1024, 1024], P('grp', None, 'row', 'col'), may hold values from 0 to 1
- grain_label: int32 [4, 1024, 1024], P('grp', 'row', 'col'), may hold values from 0 to 31
- phase_label: int32 [4, 1024, 1024], P('grp', 'row', 'col'), may hold values from 0 to 7
- grain_mobility: float32 [32], replicated, may hold values from 0.25 to 1
- stiff_index: int32 [8], replicated, may hold values from 0 to 3
- stiff_table: float32 [4, 2], replicated, may hold values from 0.5 to 2
- eigen_strain: float32 [16, 3], replicated, may hold values from -1.5 to 1.5
- macro_strain: float32 [3], replicated, may hold values from -2 to 2
Outputs:
- order_next: float32 [4, 16, 1024, 1024], P('grp', None, 'row', 'col')
- strain_field: float32 [4, 3, 1024, 1024], P('grp', None, 'row', 'col')
All inputs are finite; a program needn't handle non-finite values.
Results may differ from a plain program's by a relative error of at most 0.00014.
Values sent between devices are 32-bit elements; how exact they have to be, the bound alone decides.
No kernel may reach another device: no remote copies, remote signals or barrier semaphores. Data moves between devices by JAX's collectives and lax.ppermute only.
A program may use at most 192 MiB of HBM per device.

v0:
```python
import math

import jax
import jax.numpy as jnp
import numpy as np
from jax import lax
from jax.experimental import pallas as pl
from jax.experimental.pallas import tpu as pltpu
from jax.sharding import PartitionSpec as P


ITERS = 2
GAMMA_MIX = 1.5
KAPPA_GRAD = 1.0
STEP_TIME = 0.1
LAYER_COUPLE = 0.5
LAMBDA_REF = 1.25
SHEAR_REF = 1.25
BETA_REF = (LAMBDA_REF + SHEAR_REF) / (SHEAR_REF * (LAMBDA_REF + 2.0 * SHEAR_REF))
STRIP = 8
LANES = 128
RADIX = 4
VMEM_LIMIT = 56 * 1024 * 1024


def split3(value):
    high = value.astype(jnp.bfloat16)
    low = (value - high.astype(jnp.float32)).astype(jnp.bfloat16)
    return high, low


def dot3(left, right, dims):
    left_high, left_low = left
    right_high, right_low = right

    def product(a, b):
        return lax.dot_general(a, b, (dims, ((), ())), preferred_element_type=jnp.float32)

    return product(left_high, right_high) + (
        product(left_high, right_low) + product(left_low, right_high)
    )


def shift_rows(value, before, after):
    place = lax.broadcasted_iota(jnp.int32, value.shape, 0)
    size = value.shape[0]
    upper = jnp.where(place == 0, before, pltpu.roll(value, 1, 0))
    lower = jnp.where(place == size - 1, after, pltpu.roll(value, size - 1, 0))
    return upper, lower


def shift_cols(value, before, after):
    size = value.shape[1]
    lanes = min(size, LANES)
    place = lax.broadcasted_iota(jnp.int32, (value.shape[0], lanes), 1)
    left = pltpu.roll(value, 1, 1)
    right = pltpu.roll(value, size - 1, 1)
    head = jnp.where(place == 0, before, left[:, :lanes])
    tail = jnp.where(place == lanes - 1, after, right[:, size - lanes :])
    if size == lanes:
        return head, tail
    return (
        jnp.concatenate([head, left[:, lanes:]], axis=1),
        jnp.concatenate([right[:, : size - lanes], tail], axis=1),
    )


def put_lane(packed, lane, column):
    place = lax.broadcasted_iota(jnp.int32, packed.shape, 1)
    return jnp.where(place == lane, column, packed)


def prepare_kernel(
    grain, phase, top_rows, bottom_rows, left, right, speeds, index, table,
    mobility, stiff, edge_up, edge_dn, edge_col,
):
    count, rows = left.shape[1], left.shape[2]
    width = left.shape[3]
    labels = grain[0]
    speed = jnp.zeros(labels.shape, jnp.float32)
    for entry in range(speeds.shape[0]):
        speed = jnp.where(labels == entry, speeds[entry], speed)
    mobility[0] = speed
    labels = phase[0]
    lam = jnp.zeros(labels.shape, jnp.float32)
    shear = jnp.zeros(labels.shape, jnp.float32)
    for entry in range(index.shape[0]):
        match = labels == entry
        lam = jnp.where(match, table[index[entry], 0], lam)
        shear = jnp.where(match, table[index[entry], 1], shear)
    stiff[0, 0] = lam
    stiff[0, 1] = shear
    packed = jnp.zeros((rows, LANES), jnp.float32)
    for i in range(count):
        packed = put_lane(packed, i, left[0, i, :, 0:1])
        packed = put_lane(packed, count + 1 + i, right[0, i, :, width - 1 : width])
    packed = put_lane(packed, count, speed[:, 0:1])
    packed = put_lane(packed, 2 * count + 1, speed[:, speed.shape[1] - 1 :])
    edge_col[0] = packed[:, : 2 * count + 2]
    block = pl.program_id(1)

    @pl.when(block == 0)
    def _():
        for i in range(count):
            edge_up[0, i : i + 1, :] = top_rows[0, i, 0:1, :]
            edge_dn[0, i : i + 1, :] = bottom_rows[0, i, STRIP - 1 : STRIP, :]
        edge_up[0, count : count + 1, :] = speed[0:1, :]

    @pl.when(block == pl.num_programs(1) - 1)
    def _():
        edge_dn[0, count : count + 1, :] = speed[rows - 1 : rows, :]


def run_prepare(order_field, grain_label, phase_label, grain_mobility, stiff_index, stiff_table):
    layers, count, rows, cols = order_field.shape
    block = min(rows, 8 * STRIP)
    width = min(cols, LANES)
    smem = pl.BlockSpec(memory_space=pltpu.SMEM)
    shape = jax.ShapeDtypeStruct
    return pl.pallas_call(
        prepare_kernel,
        grid=(layers, rows // block),
        in_specs=[
            pl.BlockSpec((1, block, cols), lambda l, r: (l, r, 0)),
            pl.BlockSpec((1, block, cols), lambda l, r: (l, r, 0)),
            pl.BlockSpec((1, count, STRIP, cols), lambda l, r: (l, 0, 0, 0)),
            pl.BlockSpec((1, count, STRIP, cols), lambda l, r: (l, 0, rows // STRIP - 1, 0)),
            pl.BlockSpec((1, count, block, width), lambda l, r: (l, 0, r, 0)),
            pl.BlockSpec((1, count, block, width), lambda l, r: (l, 0, r, cols // width - 1)),
            smem,
            smem,
            smem,
        ],
        out_specs=(
            pl.BlockSpec((1, block, cols), lambda l, r: (l, r, 0)),
            pl.BlockSpec((1, 2, block, cols), lambda l, r: (l, 0, r, 0)),
            pl.BlockSpec((1, count + 1, cols), lambda l, r: (l, 0, 0)),
            pl.BlockSpec((1, count + 1, cols), lambda l, r: (l, 0, 0)),
            pl.BlockSpec((1, block, 2 * count + 2), lambda l, r: (l, r, 0)),
        ),
        out_shape=(
            shape((layers, rows, cols), jnp.float32),
            shape((layers, 2, rows, cols), jnp.float32),
            shape((layers, count + 1, cols), jnp.float32),
            shape((layers, count + 1, cols), jnp.float32),
            shape((layers, rows, 2 * count + 2), jnp.float32),
        ),
        compiler_params=pltpu.CompilerParams(vmem_limit_bytes=VMEM_LIMIT),
        name="prepare",
    )(
        grain_label, phase_label, order_field, order_field, order_field, order_field,
        grain_mobility, stiff_index, stiff_table,
    )


def pack_sides(fields, out_col):
    count, rows, cols = fields.shape[1:]
    packed = jnp.zeros((rows, LANES), jnp.float32)
    for i in range(count):
        packed = put_lane(packed, i, fields[0, i, :, 0:1])
        packed = put_lane(packed, count + i, fields[0, i, :, cols - 1 : cols])
    out_col[0] = packed[:, : 2 * count]


def emit_rim(fields, out_up, out_dn, out_col):
    count, rows, _ = fields.shape[1:]
    pack_sides(fields, out_col)

    @pl.when(pl.program_id(0) == 0)
    def _():
        for i in range(count):
            out_up[0, i : i + 1, :] = fields[0, i, 0:1, :]

    @pl.when(pl.program_id(0) == pl.num_programs(0) - 1)
    def _():
        for i in range(count):
            out_dn[0, i : i + 1, :] = fields[0, i, rows - 1 : rows, :]


def stencil_kernel(has_remote, emit, waits, count, *refs):
    refs = list(refs)
    refs.pop(0)
    phi, phi_up, phi_dn, other = (refs.pop(0) for _ in range(4))
    remote = refs.pop(0) if has_remote else None
    mob, mob_up, mob_dn = (refs.pop(0) for _ in range(3))
    edge_up, edge_dn, edge_col = (refs.pop(0) for _ in range(3))
    mob_edge_up, mob_edge_dn, mob_edge_col = (refs.pop(0) for _ in range(3))
    eigen_strain = refs.pop(0)
    del refs[:waits]
    out = refs.pop(0)
    if emit:
        out_eigen, out_up, out_dn, out_col = refs
    block = pl.program_id(0)
    first = block == 0
    last = block == pl.num_programs(0) - 1
    rows, _ = phi.shape[2:]
    strips = rows // STRIP
    side = edge_col.shape[2] // 2
    mob_side = mob_edge_col.shape[2] // 2

    def strip_body(strip, carry):
        start = pl.multiple_of(strip * STRIP, STRIP)
        here = pl.ds(start, STRIP)
        at_top = strip == 0
        at_bottom = strip == strips - 1

        def before_after(main, up, dn, edge_before, edge_after):
            before = jnp.where(
                at_top,
                jnp.where(first, edge_before, up),
                main(pl.ds(jnp.maximum(start - 1, 0), 1)),
            )
            after = jnp.where(
                at_bottom,
                jnp.where(last, edge_after, dn),
                main(pl.ds(jnp.minimum(start + STRIP, rows - 1), 1)),
            )
            return before, after

        m = mob[0, here, :]
        before, after = before_after(
            lambda r: mob[0, r, :],
            mob_up[0, STRIP - 1 : STRIP, :],
            mob_dn[0, 0:1, :],
            mob_edge_up[0, count : count + 1, :],
            mob_edge_dn[0, count : count + 1, :],
        )
        m_up, m_dn = shift_rows(m, before, after)
        m_edges = mob_edge_col[0, here, :]
        m_left, m_right = shift_cols(
            m,
            m_edges[:, mob_side + count : mob_side + count + 1],
            m_edges[:, count : count + 1],
        )
        half_step = 0.5 * STEP_TIME * KAPPA_GRAD
        w_up = half_step * (m + m_up)
        w_dn = half_step * (m + m_dn)
        w_left = half_step * (m + m_left)
        w_right = half_step * (m + m_right)
        total = jnp.zeros_like(m)
        for i in range(count):
            value = phi[0, i, here, :]
            total = total + value * value
        scaled = STEP_TIME * m
        base = (
            1.0
            - (w_up + w_dn + w_left + w_right)
            + scaled * ((1.0 - 2.0 * LAYER_COUPLE) - 2.0 * GAMMA_MIX * total)
        )
        coupling = LAYER_COUPLE * scaled
        cubic = (2.0 * GAMMA_MIX - 1.0) * scaled
        if emit:
            sums = [jnp.zeros_like(m) for _ in range(3)]
        edges = edge_col[0, here, :]
        for i in range(count):
            value = phi[0, i, here, :]
            before, after = before_after(
                lambda r: phi[0, i, r, :],
                phi_up[0, i, STRIP - 1 : STRIP, :],
                phi_dn[0, i, 0:1, :],
                edge_up[0, i : i + 1, :],
                edge_dn[0, i : i + 1, :],
            )
            upper, lower = shift_rows(value, before, after)
            left, right = shift_cols(
                value, edges[:, side + i : side + i + 1], edges[:, i : i + 1]
            )
            beside = other[0, i, here, :]
            if has_remote:
                beside = beside + remote[0, i, here, :]
            result = (
                value * (base + cubic * (value * value))
                + coupling * beside
                + (w_up * upper + w_dn * lower)
                + (w_left * left + w_right * right)
            )
            out[0, i, here, :] = result
            if emit:
                square = result * result
                for c in range(3):
                    sums[c] = sums[c] + square * eigen_strain[3 * i + c]
        if emit:
            for c in range(3):
                out_eigen[c, here, :] = sums[c]
        return carry

    lax.fori_loop(0, strips, strip_body, 0)
    if emit:
        emit_rim(out, out_up, out_dn, out_col)


def rim_outputs(count, rows, cols, block):
    shape = jax.ShapeDtypeStruct
    shapes = (
        shape((1, count, rows, cols), jnp.float32),
        shape((3, rows, cols), jnp.float32),
        shape((1, count, cols), jnp.float32),
        shape((1, count, cols), jnp.float32),
        shape((1, rows, 2 * count), jnp.float32),
    )
    specs = (
        pl.BlockSpec((1, count, block, cols), lambda r, p: (0, 0, r, 0)),
        pl.BlockSpec((3, block, cols), lambda r, p: (0, r, 0)),
        pl.BlockSpec((1, count, cols), lambda r, p: (0, 0, 0)),
        pl.BlockSpec((1, count, cols), lambda r, p: (0, 0, 0)),
        pl.BlockSpec((1, block, 2 * count), lambda r, p: (0, r, 0)),
    )
    return shapes, specs


def any_specs(values):
    return [pl.BlockSpec(memory_space=pl.ANY) for _ in values]


def run_stencil(
    places, fields, other, remote, mobility, edges, mob_edges, eigen_strain, emit, after=()
):
    _, rows, cols = mobility.shape
    count = fields.shape[1]
    block = min(rows, 4 * STRIP)
    per = block // STRIP
    tops = rows // STRIP - 1
    has_remote = remote is not None
    spec = pl.BlockSpec

    def above(r):
        return jnp.maximum(r * per - 1, 0)

    def below(r):
        return jnp.minimum((r + 1) * per, tops)

    args = [fields, fields, fields, other]
    specs = [
        spec((1, count, block, cols), lambda r, p: (p[0], 0, r, 0)),
        spec((1, count, STRIP, cols), lambda r, p: (p[0], 0, above(r), 0)),
        spec((1, count, STRIP, cols), lambda r, p: (p[0], 0, below(r), 0)),
        spec((1, count, block, cols), lambda r, p: (p[1], 0, r, 0)),
    ]
    if has_remote:
        args.append(remote)
        specs.append(spec((1, count, block, cols), lambda r, p: (0, 0, r, 0)))
    args += [mobility, mobility, mobility]
    specs += [
        spec((1, block, cols), lambda r, p: (p[2], r, 0)),
        spec((1, STRIP, cols), lambda r, p: (p[2], above(r), 0)),
        spec((1, STRIP, cols), lambda r, p: (p[2], below(r), 0)),
    ]
    for group, at in ((edges, 0), (mob_edges, 2)):
        for rows_edge in group[:2]:
            args.append(rows_edge)
            specs.append(
                spec((1, rows_edge.shape[1], cols), lambda r, p, at=at: (p[at], 0, 0))
            )
        args.append(group[2])
        specs.append(
            spec((1, block, group[2].shape[2]), lambda r, p, at=at: (p[at], r, 0))
        )
    args += [eigen_strain, *after]
    specs += [spec(memory_space=pltpu.SMEM), *any_specs(after)]
    out_shape, out_specs = rim_outputs(count, rows, cols, block)
    if not emit:
        out_shape, out_specs = out_shape[0], out_specs[0]

    def kernel(*refs):
        stencil_kernel(has_remote, emit, len(after), count, *refs)

    return pl.pallas_call(
        kernel,
        grid_spec=pltpu.PrefetchScalarGridSpec(
            num_scalar_prefetch=1,
            grid=(rows // block,),
            in_specs=specs,
            out_specs=out_specs,
        ),
        out_shape=out_shape,
        compiler_params=pltpu.CompilerParams(vmem_limit_bytes=VMEM_LIMIT),
        name="stencil",
    )(places, *args)


def finish_kernel(waits, places, partial, remote, mob, eigen_strain, *refs):
    out, out_eigen, out_up, out_dn, out_col = refs[waits:]
    count, rows = out.shape[1:3]
    for start in range(0, rows, STRIP):
        here = slice(start, start + STRIP)
        coupling = (LAYER_COUPLE * STEP_TIME) * mob[0, here, :]
        sums = [jnp.zeros_like(coupling) for _ in range(3)]
        for i in range(count):
            result = partial[0, i, here, :] + coupling * remote[0, i, here, :]
            out[0, i, here, :] = result
            square = result * result
            for c in range(3):
                sums[c] = sums[c] + square * eigen_strain[3 * i + c]
        for c in range(3):
            out_eigen[c, here, :] = sums[c]
    emit_rim(out, out_up, out_dn, out_col)


def run_finish(places, partial, remote, mobility, eigen_strain, after):
    _, rows, cols = mobility.shape
    count = partial.shape[1]
    block = min(rows, 4 * STRIP)
    field = pl.BlockSpec((1, count, block, cols), lambda r, p: (0, 0, r, 0))
    out_shape, out_specs = rim_outputs(count, rows, cols, block)

    def kernel(*refs):
        finish_kernel(len(after), *refs)

    return pl.pallas_call(
        kernel,
        grid_spec=pltpu.PrefetchScalarGridSpec(
            num_scalar_prefetch=1,
            grid=(rows // block,),
            in_specs=[
                field,
                field,
                pl.BlockSpec((1, block, cols), lambda r, p: (p[2], r, 0)),
                pl.BlockSpec(memory_space=pltpu.SMEM),
                *any_specs(after),
            ],
            out_specs=out_specs,
        ),
        out_shape=out_shape,
        compiler_params=pltpu.CompilerParams(vmem_limit_bytes=VMEM_LIMIT),
        name="finish",
    )(places, partial, remote, mobility, eigen_strain, *after)


def drive_kernel(places, pre, phi, mob, stiff, eigen, eigen_strain, signs, macro, *refs):
    swaps = [(refs[2 * k], refs[2 * k + 1]) for k in range(ITERS)]
    out, out_strain = refs[-2:]
    count, rows = phi.shape[1:3]
    sign = signs[0]
    for start in range(0, rows, STRIP):
        here = slice(start, start + STRIP)
        lam = stiff[0, 0, here, :]
        shear2 = 2.0 * stiff[0, 1, here, :]
        elastic = []
        for c in range(3):
            strain = macro[c]
            for mine, theirs in swaps:
                strain = strain - (theirs[c, here, :] + sign * mine[c, here, :])
            out_strain[0, c, here, :] = strain
            elastic.append(strain - eigen[c, here, :])
        spread = lam * (elastic[0] + elastic[1])
        push = (2.0 * STEP_TIME) * mob[0, here, :]
        sigma = (
            push * (spread + shear2 * elastic[0]),
            push * (spread + shear2 * elastic[1]),
            push * (2.0 * shear2 * elastic[2]),
        )
        for i in range(count):
            force = (
                sigma[0] * eigen_strain[3 * i]
                + sigma[1] * eigen_strain[3 * i + 1]
                + sigma[2] * eigen_strain[3 * i + 2]
            )
            out[0, i, here, :] = pre[0, i, here, :] + phi[0, i, here, :] * force


def run_drive(places, pre, fields, mobility, stiff, eigen, eigen_strain, signs, macro, swaps, held):
    layers, rows, cols = mobility.shape
    count = fields.shape[1]
    block = min(rows, 4 * STRIP)
    smem = pl.BlockSpec(memory_space=pltpu.SMEM)
    field = pl.BlockSpec((1, count, block, cols), lambda r, p: (0, 0, r, 0))
    plane = pl.BlockSpec((3, block, cols), lambda r, p: (0, r, 0))
    args = [pre, fields, mobility, stiff, eigen, eigen_strain, signs, macro]
    specs = [
        field,
        field,
        pl.BlockSpec((1, block, cols), lambda r, p: (p[2], r, 0)),
        pl.BlockSpec((1, 2, block, cols), lambda r, p: (p[2], 0, r, 0)),
        plane,
        smem,
        smem,
        smem,
    ]
    for pair in swaps:
        args += list(pair)
        specs += [plane, plane]
    aliases = {}
    if held is not None:
        aliases = {1 + len(args): 0, 2 + len(args): 1}
        args += list(held)
        specs += any_specs(held)
    return pl.pallas_call(
        drive_kernel,
        grid_spec=pltpu.PrefetchScalarGridSpec(
            num_scalar_prefetch=1,
            grid=(rows // block,),
            in_specs=specs,
            out_specs=(
                pl.BlockSpec((1, count, block, cols), lambda r, p: (p[2], 0, r, 0)),
                pl.BlockSpec((1, 3, block, cols), lambda r, p: (p[2], 0, r, 0)),
            ),
        ),
        out_shape=(
            jax.ShapeDtypeStruct((layers, count, rows, cols), jnp.float32),
            jax.ShapeDtypeStruct((layers, 3, rows, cols), jnp.float32),
        ),
        input_output_aliases=aliases,
        compiler_params=pltpu.CompilerParams(vmem_limit_bytes=VMEM_LIMIT),
        name="drive",
    )(places, *args)


def forward_kernel(has_swap, parts, waits, *refs):
    refs = list(refs)
    refs.pop(0)
    signs, macro, stiff, stiff_far, eigen, eigen_far = (refs.pop(0) for _ in range(6))
    swap = (refs.pop(0), refs.pop(0)) if has_swap else None
    high, low = refs.pop(0), refs.pop(0)
    out, flat = refs[waits:]
    rows = eigen.shape[1]
    sign = signs[0]
    near = []
    far = []
    for c in range(3):
        strain = strain_far = macro[c]
        if has_swap:
            mine = swap[0][c]
            theirs = swap[1][c]
            strain = strain - (theirs + sign * mine)
            strain_far = strain_far - (mine - sign * theirs)
        near.append(strain - eigen[c])
        far.append(strain_far - eigen_far[c])

    def stress(elastic, table):
        lam = table[0, 0]
        shear2 = 2.0 * table[0, 1]
        spread = lam * (elastic[0] + elastic[1])
        return (
            spread + shear2 * elastic[0],
            spread + shear2 * elastic[1],
            shear2 * elastic[2],
        )

    near = stress(near, stiff)
    far = stress(far, stiff_far)
    for c in range(3):
        flat[c * rows : (c + 1) * rows, :] = far[c] + sign * near[c]
    result = dot3((high[0], low[0]), split3(flat[...]), ((1,), (1,)))
    width = result.shape[0] // 2
    part = width // parts
    for q in range(parts):
        for side in range(2):
            at = side * width + q * part
            for c in range(3):
                out[q, side, c] = result[at : at + part, c * rows : (c + 1) * rows]


def run_forward(places, signs, macro, stiff, stiff_far, eigen, eigen_far, swap, waves, parts, after):
    rows, cols = eigen.shape[1:]
    width = waves[0].shape[1]
    smem = pl.BlockSpec(memory_space=pltpu.SMEM)
    plane = pl.BlockSpec((3, rows, cols), lambda g, p: (0, 0, 0))
    table = pl.BlockSpec((1, 2, rows, cols), lambda g, p: (p[2], 0, 0, 0))
    wave = pl.BlockSpec((1, width, cols), lambda g, p: (0, 0, 0))
    args = [signs, macro, stiff, stiff_far, eigen, eigen_far]
    specs = [smem, smem, table, table, plane, plane]
    if swap is not None:
        args += list(swap)
        specs += [plane, plane]
    args += list(waves)
    specs += [wave, wave]
    args += list(after)
    specs += any_specs(after)
    shape = (parts, 2, 3, width // (2 * parts), rows)

    def kernel(*refs):
        forward_kernel(swap is not None, parts, len(after), *refs)

    return pl.pallas_call(
        kernel,
        grid_spec=pltpu.PrefetchScalarGridSpec(
            num_scalar_prefetch=1,
            grid=(1,),
            in_specs=specs,
            out_specs=pl.BlockSpec(shape, lambda g, p: (0, 0, 0, 0, 0)),
            scratch_shapes=[pltpu.VMEM((3 * rows, cols), jnp.float32)],
        ),
        out_shape=jax.ShapeDtypeStruct(shape, jnp.float32),
        compiler_params=pltpu.CompilerParams(vmem_limit_bytes=VMEM_LIMIT),
        name="forward_columns",
    )(places, *args)


def inverse_kernel(recv, high, low, *refs):
    out, flat = refs[-2:]
    parts, _, _, part, rows = recv.shape
    width = parts * part
    for q in range(parts):
        for side in range(2):
            at = side * width + q * part
            for c in range(3):
                flat[at : at + part, c * rows : (c + 1) * rows] = recv[q, side, c]
    result = dot3(split3(flat[...]), (high[0], low[0]), ((0,), (0,)))
    for c in range(3):
        out[c] = result[c * rows : (c + 1) * rows, :]


def run_inverse(recv, waves, after):
    _, _, _, _, rows = recv.shape
    _, width, cols = waves[0].shape
    whole = pl.BlockSpec(memory_space=pltpu.VMEM)
    return pl.pallas_call(
        inverse_kernel,
        in_specs=[whole, whole, whole, *any_specs(after)],
        out_specs=whole,
        out_shape=jax.ShapeDtypeStruct((3, rows, cols), jnp.float32),
        scratch_shapes=[pltpu.VMEM((width, 3 * rows), jnp.float32)],
        compiler_params=pltpu.CompilerParams(vmem_limit_bytes=VMEM_LIMIT),
        name="inverse_columns",
    )(recv, *waves, *after)


def rows_kernel(rows_total, cols_total, places, recv, turns, high, low, *refs):
    out, held = refs[-2:]
    parts, _, _, part, rows = recv.shape
    span = rows_total // RADIX

    def turn(c):
        return turns[2 * c : 2 * c + 1, :], turns[2 * c + 1 : 2 * c + 2, :]

    def at(c, n):
        start = (c * 3 + n) * part
        return slice(start, start + part)

    def gather(side, n):
        if parts == 1:
            return recv[0, side, n]
        return jnp.concatenate([recv[s, side, n] for s in range(parts)], axis=1)

    for n in range(3):
        real = gather(0, n)
        imag = gather(1, n)
        r = [real[:, a * span : (a + 1) * span] for a in range(RADIX)]
        m = [imag[:, a * span : (a + 1) * span] for a in range(RADIX)]
        r02, r13, d02, d13 = r[0] + r[2], r[1] + r[3], r[0] - r[2], r[1] - r[3]
        m02, m13, e02, e13 = m[0] + m[2], m[1] + m[3], m[0] - m[2], m[1] - m[3]
        mixed = (
            (r02 + r13, m02 + m13),
            (d02 + e13, e02 - d13),
            (r02 - r13, m02 - m13),
            (d02 - e13, e02 + d13),
        )
        for c in range(RADIX):
            x, y = mixed[c]
            if c:
                cosine, sine = turn(c)
                x, y = x * cosine + y * sine, y * cosine - x * sine
            held[at(c, n), :span] = x
            held[at(c, n), span:] = y
    wave = (high[...], low[...])
    held[...] = dot3(split3(held[...]), wave, ((1,), (0,)))

    lanes = lax.broadcasted_iota(jnp.int32, (part, 2 * span), 1)
    lanes = jnp.where(lanes >= span, lanes - span, lanes)
    lines = lax.broadcasted_iota(jnp.int32, (part, 2 * span), 0)
    freq_col = 2 * (places[3] * part + lines) + places[4]
    signed_col = freq_col.astype(jnp.float32)
    scale = jnp.where(freq_col == 0, 1.0, 2.0) * (1.0 / (rows_total * cols_total))
    for c in range(RADIX):
        freq_row = RADIX * lanes + c
        signed_row = jnp.where(
            freq_row >= rows_total // 2, freq_row - rows_total, freq_row
        ).astype(jnp.float32)
        radius = signed_row * signed_row + signed_col * signed_col
        keep = (freq_row != rows_total // 2) & (freq_col != cols_total // 2)
        inverse = jnp.where(keep & (radius > 0.0), 1.0 / jnp.maximum(radius, 1.0), 0.0)
        n11 = signed_row * signed_row * inverse
        n12 = signed_row * signed_col * inverse
        n22 = signed_col * signed_col * inverse
        s_rr = held[at(c, 0), :]
        s_cc = held[at(c, 1), :]
        s_rc = held[at(c, 2), :]
        along_r = s_rr * n11 + s_rc * n12
        along_c = s_rc * n12 + s_cc * n22
        normal = BETA_REF * (along_r + along_c)
        cross = 0.5 * (n12 * (s_rr + s_cc) + s_rc * (n11 + n22))
        held[at(c, 0), :] = scale * (along_r * (1.0 / SHEAR_REF) - n11 * normal)
        held[at(c, 1), :] = scale * (along_c * (1.0 / SHEAR_REF) - n22 * normal)
        held[at(c, 2), :] = scale * (cross * (1.0 / SHEAR_REF) - n12 * normal)
    held[...] = dot3(split3(held[...]), wave, ((1,), (1,)))
    for n in range(3):
        v = []
        for c in range(RADIX):
            x = held[at(c, n), :span]
            y = held[at(c, n), span:]
            if c:
                cosine, sine = turn(c)
                x, y = x * cosine - y * sine, y * cosine + x * sine
            v.append((x, y))
        r02, r13 = v[0][0] + v[2][0], v[1][0] + v[3][0]
        d02, d13 = v[0][0] - v[2][0], v[1][0] - v[3][0]
        m02, m13 = v[0][1] + v[2][1], v[1][1] + v[3][1]
        e02, e13 = v[0][1] - v[2][1], v[1][1] - v[3][1]
        real = jnp.concatenate([r02 + r13, d02 - e13, r02 - r13, d02 + e13], axis=1)
        imag = jnp.concatenate([m02 + m13, e02 + d13, m02 - m13, e02 - d13], axis=1)
        for s in range(parts):
            out[s, 0, n] = real[:, s * rows : (s + 1) * rows]
            out[s, 1, n] = imag[:, s * rows : (s + 1) * rows]


def row_wave(span):
    ids = np.arange(span)
    angle = (np.outer(ids, ids) % span) * (2.0 * math.pi / span)
    cosine, sine = np.cos(angle), np.sin(angle)
    full = np.block([[cosine, -sine], [sine, cosine]]).astype(np.float32)
    high = full.astype(jnp.bfloat16)
    low = (full - high.astype(np.float32)).astype(jnp.bfloat16)
    turns = []
    for c in range(RADIX):
        angle = ids * c * (2.0 * math.pi / (RADIX * span))
        turns += [np.cos(angle), np.sin(angle)]
    return np.stack(turns).astype(np.float32), high, low


def run_rows(places, recv, tables, rows_total, cols_total, after):
    parts, _, _, part, rows = recv.shape
    dense = rows % 128 == 0
    if not dense:
        recv = jnp.transpose(recv, (1, 2, 3, 0, 4)).reshape(1, 2, 3, part, rows_total)
    span = rows_total // RADIX

    def kernel(*refs):
        rows_kernel(rows_total, cols_total, *refs)

    whole = pl.BlockSpec(memory_space=pltpu.VMEM)
    out = pl.pallas_call(
        kernel,
        in_specs=[pl.BlockSpec(memory_space=pltpu.SMEM), whole, whole, whole, whole, *any_specs(after)],
        out_specs=whole,
        out_shape=jax.ShapeDtypeStruct(recv.shape, jnp.float32),
        scratch_shapes=[pltpu.VMEM((RADIX * 3 * part, 2 * span), jnp.float32)],
        compiler_params=pltpu.CompilerParams(vmem_limit_bytes=VMEM_LIMIT),
        name="row_lines",
    )(places, recv, *tables, *after)
    if not dense:
        out = jnp.transpose(out.reshape(2, 3, part, parts, rows), (3, 0, 1, 2, 4))
    return out


def column_waves(freqs, ids, length):
    product = freqs[:, None] * ids[None, :] % length
    angle = product.astype(jnp.float32) * (2.0 * math.pi / length)
    full = jnp.concatenate([jnp.cos(angle), -jnp.sin(angle)], axis=0)[None]
    rounded = lax.reduce_precision(full, 8, 7)
    return rounded.astype(jnp.bfloat16), (full - rounded).astype(jnp.bfloat16)


def body(
    order_field,
    grain_label,
    phase_label,
    grain_mobility,
    stiff_index,
    stiff_table,
    eigen_strain,
    macro_strain,
):
    layers, _, rows, cols = order_field.shape
    parts = lax.axis_size("row")
    if lax.axis_size("grp") != 2 or layers != 2 or lax.axis_size("col") != 2:
        raise ValueError("unsupported split")
    group = lax.axis_index("grp").astype(jnp.int32)
    row_place = lax.axis_index("row").astype(jnp.int32)
    col_place = lax.axis_index("col").astype(jnp.int32)
    rows_total = rows * parts
    cols_total = cols * 2
    inner = group
    outer = 1 - group
    swap_pairs = [(0, 1), (1, 0)]
    ring_up = [(i, (i + 1) % parts) for i in range(parts)]
    ring_down = [(j, i) for i, j in ring_up]

    def swap_cols(value):
        return lax.ppermute(value, "col", swap_pairs)

    def swap_layers(value):
        return lax.ppermute(value, "grp", swap_pairs)

    remote_field = swap_layers(lax.dynamic_slice_in_dim(order_field, outer, 1, 0))

    mobility, stiff, top, bottom, sides = run_prepare(
        order_field, grain_label, phase_label, grain_mobility, stiff_index, stiff_table
    )

    def move_edges(top, bottom, sides):
        return (
            lax.ppermute(bottom, "row", ring_up),
            lax.ppermute(top, "row", ring_down),
            swap_cols(sides),
        )

    edges = move_edges(top, bottom, sides)
    stiff_far = swap_cols(stiff)
    signs = (1 - 2 * col_place).astype(jnp.float32)[None]
    strain_table = eigen_strain.reshape(-1)
    waves = column_waves(
        2 * jnp.arange(cols_total // 4, dtype=jnp.int32) + col_place,
        jnp.arange(cols, dtype=jnp.int32),
        cols_total,
    )
    tables = row_wave(rows_total // RADIX)

    def places(phi_at, other_at, layer):
        zero = jnp.zeros((), jnp.int32)
        return jnp.stack([zero + phi_at, zero + other_at, layer, row_place, col_place])

    def exchange(value):
        return lax.all_to_all(value, "row", split_axis=0, concat_axis=0, tiled=True)

    def stencil(fields, phi_at, other, other_at, remote, layer, own_edges, emit, after=()):
        return run_stencil(
            places(phi_at, other_at, layer),
            fields,
            other,
            remote,
            mobility,
            own_edges,
            edges,
            strain_table,
            emit,
            after,
        )

    here = {"inner": places(0, 0, inner), "outer": places(0, 0, outer)}

    def forward(name, eigen, eigen_far, swap, after=()):
        return run_forward(
            here[name],
            signs,
            macro_strain,
            stiff,
            stiff_far,
            eigen,
            eigen_far,
            swap,
            waves,
            parts,
            after,
        )

    def lines(name, recv, after=()):
        return run_rows(here[name], recv, tables, rows_total, cols_total, after)

    def columns(recv, after=()):
        mine = run_inverse(recv, waves, after)
        return mine, swap_cols(mine)

    def drive(name, pre, fields, eigen, swaps, held):
        return run_drive(
            here[name],
            pre,
            fields,
            mobility,
            stiff,
            eigen,
            strain_table,
            signs,
            macro_strain,
            swaps,
            held,
        )

    middle_inner, eigen_inner, *rim_inner = stencil(
        order_field, inner, order_field, outer, None, inner, edges, True, waves
    )
    far_inner = swap_cols(eigen_inner)
    sent = exchange(forward("inner", eigen_inner, far_inner, None))
    partial = stencil(order_field, outer, order_field, inner, None, outer, edges, False)
    edges_inner = move_edges(*rim_inner)
    back = exchange(lines("inner", sent, (partial,)))
    swaps_inner = [columns(back)]
    held_back = forward("inner", eigen_inner, far_inner, swaps_inner[0])
    sent_inner = exchange(held_back)

    middle_outer, eigen_outer, *rim_outer = run_finish(
        here["outer"], partial, remote_field, mobility, strain_table, (held_back,)
    )
    far_outer = swap_cols(eigen_outer)
    first_outer = forward("outer", eigen_outer, far_outer, None)
    sent_outer = exchange(first_outer)
    remote_middle = swap_layers(middle_outer)
    edges_outer = move_edges(*rim_outer)
    spread_inner = lines("inner", sent_inner)
    back_inner = exchange(spread_inner)
    pre_inner = stencil(middle_inner, 0, middle_outer, 0, None, inner, edges_inner, False)
    spread_outer = lines("outer", sent_outer, (pre_inner,))
    back_outer = exchange(spread_outer)
    swaps_inner.append(columns(back_inner))
    swaps_outer = [columns(back_outer)]
    sent_outer = exchange(forward("outer", eigen_outer, far_outer, swaps_outer[0]))
    held = drive("inner", pre_inner, middle_inner, eigen_inner, swaps_inner, None)
    back_outer = exchange(lines("outer", sent_outer, held))
    pre_outer = stencil(
        middle_outer, 0, middle_inner, 0, remote_middle, outer, edges_outer, False
    )
    swaps_outer.append(columns(back_outer, (pre_outer,)))
    return drive("outer", pre_outer, middle_outer, eigen_outer, swaps_outer, held)


def solution(mesh):
    return jax.shard_map(
        body,
        mesh=mesh,
        in_specs=(
            P("grp", None, "row", "col"),
            P("grp", "row", "col"),
            P("grp", "row", "col"),
            P(),
            P(),
            P(),
            P(),
            P(),
        ),
        out_specs=(P("grp", None, "row", "col"), P("grp", None, "row", "col")),
        check_vma=False,
    )
```

profile of v0, /device:TPU:0, one launch (start us, length us, event | category | flops | bytes accessed | tf_op | source)
XLA Modules:
  0.0 337.3 jit_solution(16456265791829014529)
XLA Ops:
  2.0 6.0 %prepare.1 = (f32[2,128,512]{2,1,0:T(8,128)}, f32[2,2,128,512]{3,2,1,0:T(8,128)}, f32[2,17,512]{2,1,0:T(8,128)}, f32[2,17,512]{2,1,0:T(8,128)}, f32[2,128,34]{2,1,0:T(8,128)}) custom-call(s32[2,128,512]{2,1,0:T(8,128)} %grain.1, s32[2,128,512]{2,1,0:T(8,128)} %phase.1, f32[2,16,128,512]{3,2,1,0:T(8,128)} %refs_4_.7, f32[2,16,128,512]{3,2,1,0:T(8,128)} %refs_4_.7, ...), custom_call_target="tpu_custom_call" | custom-call | tf_op jit(solution)/shard_map/prepare/pallas_call | solution.py:120
  8.0 3.0 collective-permute-start
  11.0 3.1 collective-permute-start.1
  14.7 2.1 cosine_bitcast_fusion
  20.1 12.0 %stencil.5 = (f32[1,16,128,512]{3,2,1,0:T(8,128)}, f32[3,128,512]{2,1,0:T(8,128)}, f32[1,16,512]{2,1,0:T(8,128)}, f32[1,16,512]{2,1,0:T(8,128)}, f32[1,128,32]{2,1,0:T(8,128)}) custom-call(s32[5]{0:T(128)} %stack.23.refs_0_, f32[2,16,128,512]{3,2,1,0:T(8,128)} %refs_4_.7, f32[2,16,128,512]{3,2,1,0:T(8,128)} %refs_4_.7, f32[2,16,128,512]{3,2,1,0:T(8,128)} %refs_4_.7, ...), custom_call_target="tpu_custom_call" | custom-call | tf_op jit(solution)/shard_map/stencil/pallas_call | solution.py:367
  32.2 4.8 %constant_dynamic-slice_fusion = f32[1,16,128,512]{3,2,1,0:T(8,128)} fusion(f32[2,16,128,512]{3,2,1,0:T(8,128)} %refs_4_.7, s32[]{:T(128)S(6)} %select_n.28), kind=kLoop, calls=%fused_computation.22 | loop fusion | bytes 8388612 | tf_op jit(solution)/shard_map/dynamic_slice | solution.py:784
  40.6 4.7 %forward_columns.4 = f32[8,2,3,32,128]{4,3,2,1,0:T(8,128)} custom-call(s32[5]{0:T(128)} %get-tuple-element.40.refs_0_.places, f32[1]{0:T(128)} %bitcast.4.refs_1_.signs, f32[3]{0:T(128)} %macro.3, f32[2,2,128,512]{3,2,1,0:T(8,128)} %get-tuple-element.23.refs_3_.stiff, f32[2,2,128,512]{3,2,1,0:T(8,128)} %copy-done, ...), custom_call_target="tpu_custom_call" | custom-call | tf_op jit(solution)/shard_map/forward_columns/pallas_call | solution.py:574
  45.2 3.5 %all-to-all-start = ((f32[8,2,3,32,128]{4,3,2,1,0:T(8,128)}), f32[8,2,3,32,128]{4,3,2,1,0:T(8,128)S(1)}, u32[]{:S(2)}, u32[]{:S(2)}) async-start(f32[8,2,3,32,128]{4,3,2,1,0:T(8,128)} %forward_columns.4), calls=%async_computation | async-start | bytes 1572864 | tf_op jit(solution)/shard_map/all_to_all | solution.py:813
  49.4 10.8 %stencil.4.refs_5_.refs_1_ = f32[1,16,128,512]{3,2,1,0:T(8,128)} custom-call(s32[5]{0:T(128)} %stack.21.refs_0_, f32[2,16,128,512]{3,2,1,0:T(8,128)} %refs_4_.7, f32[2,16,128,512]{3,2,1,0:T(8,128)} %refs_4_.7, f32[2,16,128,512]{3,2,1,0:T(8,128)} %refs_4_.7, f32[2,16,128,512]{3,2,1,0:T(8,128)} %refs_4_.7, ...), custom_call_target="tpu_custom_call" | custom-call | tf_op jit(solution)/shard_map/stencil/pallas_call | solution.py:367
  60.2 9.3 %all-to-all-done.refs_1_ = f32[8,2,3,32,128]{4,3,2,1,0:T(8,128)S(1)} async-done(((f32[8,2,3,32,128]{4,3,2,1,0:T(8,128)}), f32[8,2,3,32,128]{4,3,2,1,0:T(8,128)S(1)}, u32[]{:S(2)}, u32[]{:S(2)}) %all-to-all-start) | async-done | bytes 786464 | tf_op jit(solution)/shard_map/all_to_all | solution.py:813
  70.4 4.1 %row_lines.4 = f32[8,2,3,32,128]{4,3,2,1,0:T(8,128)} custom-call(s32[5]{0:T(128)} %get-tuple-element.40.refs_0_.places, f32[8,2,3,32,128]{4,3,2,1,0:T(8,128)} %copy-done.12, f32[8,256]{1,0:T(8,128)} %constant.44.clone.refs_2_, bf16[512,512]{1,0:T(8,128)(2,1)} %constant.45.clone.refs_3_, bf16[512,512]{1,0:T(8,128)(2,1)} %constant.46.clone.refs_4_, ...), custom_call_target="tpu_custom_call" | custom-call | tf_op jit(solution)/shard_map/row_lines/pallas_call | solution.py:731
  74.6 24.1 %all_to_all.40.recv = f32[8,2,3,32,128]{4,3,2,1,0:T(8,128)} all-to-all(f32[8,2,3,32,128]{4,3,2,1,0:T(8,128)} %row_lines.4), channel_id=1, replica_groups=mesh['grp'=2,'row'=8,'col'=2] {'row'}, dimensions={0} | all-to-all | bytes 1572864 | tf_op jit(solution)/shard_map/all_to_all | solution.py:813
  98.6 3.2 inverse_columns.4.refs_7_.refs_0_
  101.8 2.5 collective-permute-done.6.refs_8_.refs_1_
  105.2 5.3 %forward_columns.5.refs_5_ = f32[8,2,3,32,128]{4,3,2,1,0:T(8,128)} custom-call(s32[5]{0:T(128)} %get-tuple-element.40.refs_0_.places, f32[1]{0:T(128)} %bitcast.4.refs_1_.signs, f32[3]{0:T(128)} %macro.3, f32[2,2,128,512]{3,2,1,0:T(8,128)} %get-tuple-element.23.refs_3_.stiff, f32[2,2,128,512]{3,2,1,0:T(8,128)} %copy-done, ...), custom_call_target="tpu_custom_call" | custom-call | tf_op jit(solution)/shard_map/forward_columns/pallas_call | solution.py:574
  110.5 19.7 %collective-permute-done.3.refs_2_ = f32[1,16,128,512]{3,2,1,0:T(8,128)} collective-permute-done((f32[1,16,128,512]{3,2,1,0:T(8,128)}, f32[1,16,128,512]{3,2,1,0:T(8,128)}, u32[]{:S(2)}, u32[]{:S(2)}) %collective-permute-start.3) | collective-permute-done | bytes 4194336 | tf_op jit(solution)/shard_map/ppermute | solution.py:782
  130.2 7.4 %finish.1 = (f32[1,16,128,512]{3,2,1,0:T(8,128)}, f32[3,128,512]{2,1,0:T(8,128)}, f32[1,16,512]{2,1,0:T(8,128)}, f32[1,16,512]{2,1,0:T(8,128)}, f32[1,128,32]{2,1,0:T(8,128)}) custom-call(s32[5]{0:T(128)} %get-tuple-element.41.refs_0_.places, f32[1,16,128,512]{3,2,1,0:T(8,128)} %stencil.4.refs_5_.refs_1_, ...), custom_call_target="tpu_custom_call" | custom-call | tf_op jit(solution)/shard_map/finish/pallas_call | solution.py:409
  137.8 2.5 collective-permute-done.11.refs_6_
  141.1 4.7 %forward_columns.6 = f32[8,2,3,32,128]{4,3,2,1,0:T(8,128)} custom-call(s32[5]{0:T(128)} %get-tuple-element.41.refs_0_.places, f32[1]{0:T(128)} %bitcast.4.refs_1_.signs, f32[3]{0:T(128)} %macro.3, f32[2,2,128,512]{3,2,1,0:T(8,128)} %get-tuple-element.23.refs_3_.stiff, f32[2,2,128,512]{3,2,1,0:T(8,128)} %copy-done, ...), custom_call_target="tpu_custom_call" | custom-call | tf_op jit(solution)/shard_map/forward_columns/pallas_call | solution.py:574
  145.8 24.9 %all_to_all.41.refs_1_ = f32[8,2,3,32,128]{4,3,2,1,0:T(8,128)} all-to-all(f32[8,2,3,32,128]{4,3,2,1,0:T(8,128)} %forward_columns.6), channel_id=1, replica_groups=mesh['grp'=2,'row'=8,'col'=2] {'row'}, dimensions={0} | all-to-all | bytes 1572864 | tf_op jit(solution)/shard_map/all_to_all | solution.py:813
  170.7 3.7 %all-to-all-start.5 = ((f32[8,2,3,32,128]{4,3,2,1,0:T(8,128)}), f32[8,2,3,32,128]{4,3,2,1,0:T(8,128)S(1)}, u32[]{:S(2)}, u32[]{:S(2)}) async-start(f32[8,2,3,32,128]{4,3,2,1,0:T(8,128)} %forward_columns.5.refs_5_), calls=%async_computation.5 | async-start | bytes 1572864 | tf_op jit(solution)/shard_map/all_to_all | solution.py:813
  174.4 1.9 collective-permute-start.12
  176.4 2.9 collective-permute-start.13
  180.5 12.4 %collective-permute-done.12.refs_8_ = f32[1,16,512]{2,1,0:T(8,128)S(1)} collective-permute-done((f32[1,16,512]{2,1,0:T(8,128)S(1)}, f32[1,16,512]{2,1,0:T(8,128)S(1)}, u32[]{:S(2)}, u32[]{:S(2)}) %collective-permute-start.12) | collective-permute-done | bytes 32800 | tf_op jit(solution)/shard_map/ppermute | solution.py:792
  193.6 10.8 %stencil.7.refs_5_.pre = f32[1,16,128,512]{3,2,1,0:T(8,128)} custom-call(s32[5]{0:T(128)} %get-tuple-element.40.refs_0_.places, f32[1,16,128,512]{3,2,1,0:T(8,128)} %get-tuple-element.26.refs_4_.refs_1_.refs_2_.refs_3_.phi, f32[1,16,128,512]{3,2,1,0:T(8,128)} %get-tuple-element.26.refs_4_.refs_1_.refs_2_.refs_3_.phi, ...), custom_call_target="tpu_custom_call" | custom-call | tf_op jit(solution)/shard_map/stencil/pallas_call | solution.py:367
  204.4 4.1 %row_lines.5 = f32[8,2,3,32,128]{4,3,2,1,0:T(8,128)} custom-call(s32[5]{0:T(128)} %get-tuple-element.41.refs_0_.places, f32[8,2,3,32,128]{4,3,2,1,0:T(8,128)} %all_to_all.41.refs_1_, f32[8,256]{1,0:T(8,128)} %constant.44.clone.refs_2_, bf16[512,512]{1,0:T(8,128)(2,1)} %constant.45.clone.refs_3_, bf16[512,512]{1,0:T(8,128)(2,1)} %constant.46.clone.refs_4_, ...), custom_call_target="tpu_custom_call" | custom-call | tf_op jit(solution)/shard_map/row_lines/pallas_call | solution.py:731
  208.5 5.2 %all-to-all-start.3 = ((f32[8,2,3,32,128]{4,3,2,1,0:T(8,128)}), f32[8,2,3,32,128]{4,3,2,1,0:T(8,128)S(1)}, u32[]{:S(2)}, u32[]{:S(2)}) async-start(f32[8,2,3,32,128]{4,3,2,1,0:T(8,128)} %row_lines.5), calls=%async_computation.3 | async-start | bytes 1572864 | tf_op jit(solution)/shard_map/all_to_all | solution.py:813
  215.4 4.1 %row_lines.6 = f32[8,2,3,32,128]{4,3,2,1,0:T(8,128)} custom-call(s32[5]{0:T(128)} %get-tuple-element.40.refs_0_.places, f32[8,2,3,32,128]{4,3,2,1,0:T(8,128)} %copy-done.5, f32[8,256]{1,0:T(8,128)} %constant.44.clone.refs_2_, bf16[512,512]{1,0:T(8,128)(2,1)} %constant.45.clone.refs_3_, bf16[512,512]{1,0:T(8,128)(2,1)} %constant.46.clone.refs_4_), custom_call_target="tpu_custom_call" | custom-call | tf_op jit(solution)/shard_map/row_lines/pallas_call | solution.py:731
  219.5 14.5 %all-to-all-done.3.recv = f32[8,2,3,32,128]{4,3,2,1,0:T(8,128)S(1)} async-done(((f32[8,2,3,32,128]{4,3,2,1,0:T(8,128)}), f32[8,2,3,32,128]{4,3,2,1,0:T(8,128)S(1)}, u32[]{:S(2)}, u32[]{:S(2)}) %all-to-all-start.3) | async-done | bytes 786464 | tf_op jit(solution)/shard_map/all_to_all | solution.py:813
  234.0 3.5 %all-to-all-start.6 = ((f32[8,2,3,32,128]{4,3,2,1,0:T(8,128)}), f32[8,2,3,32,128]{4,3,2,1,0:T(8,128)S(1)}, u32[]{:S(2)}, u32[]{:S(2)}) async-start(f32[8,2,3,32,128]{4,3,2,1,0:T(8,128)} %row_lines.6), calls=%async_computation.6 | async-start | bytes 1572864 | tf_op jit(solution)/shard_map/all_to_all | solution.py:813
  237.6 3.1 inverse_columns.5.refs_7_.refs_0_
  240.7 2.5 collective-permute-done.15.refs_8_.refs_1_
  244.1 5.3 %forward_columns.7 = f32[8,2,3,32,128]{4,3,2,1,0:T(8,128)} custom-call(s32[5]{0:T(128)} %get-tuple-element.41.refs_0_.places, f32[1]{0:T(128)} %bitcast.4.refs_1_.signs, f32[3]{0:T(128)} %macro.3, f32[2,2,128,512]{3,2,1,0:T(8,128)} %get-tuple-element.23.refs_3_.stiff, f32[2,2,128,512]{3,2,1,0:T(8,128)} %copy-done, ...), custom_call_target="tpu_custom_call" | custom-call | tf_op jit(solution)/shard_map/forward_columns/pallas_call | solution.py:574
  249.4 8.6 %all-to-all-done.6.recv = f32[8,2,3,32,128]{4,3,2,1,0:T(8,128)S(1)} async-done(((f32[8,2,3,32,128]{4,3,2,1,0:T(8,128)}), f32[8,2,3,32,128]{4,3,2,1,0:T(8,128)S(1)}, u32[]{:S(2)}, u32[]{:S(2)}) %all-to-all-start.6) | async-done | bytes 786464 | tf_op jit(solution)/shard_map/all_to_all | solution.py:813
  257.9 3.5 %all-to-all-start.4 = ((f32[8,2,3,32,128]{4,3,2,1,0:T(8,128)}), f32[8,2,3,32,128]{4,3,2,1,0:T(8,128)S(1)}, u32[]{:S(2)}, u32[]{:S(2)}) async-start(f32[8,2,3,32,128]{4,3,2,1,0:T(8,128)} %forward_columns.7), calls=%async_computation.4 | async-start | bytes 1572864 | tf_op jit(solution)/shard_map/all_to_all | solution.py:813
  261.5 3.1 inverse_columns.6.refs_2_
  264.7 2.5 collective-permute-done.16.refs_3_
  268.1 8.1 %drive.2 = (f32[2,16,128,512]{3,2,1,0:T(8,128)}, f32[2,3,128,512]{3,2,1,0:T(8,128)}) custom-call(s32[5]{0:T(128)} %get-tuple-element.40.refs_0_.places, f32[1,16,128,512]{3,2,1,0:T(8,128)} %stencil.7.refs_5_.pre, f32[1,16,128,512]{3,2,1,0:T(8,128)} %get-tuple-element.26.refs_4_.refs_1_.refs_2_.refs_3_.phi, ...), custom_call_target="tpu_custom_call" | custom-call | tf_op jit(solution)/shard_map/drive/pallas_call | solution.py:487
  276.2 5.7 %all-to-all-done.4.refs_1_ = f32[8,2,3,32,128]{4,3,2,1,0:T(8,128)S(1)} async-done(((f32[8,2,3,32,128]{4,3,2,1,0:T(8,128)}), f32[8,2,3,32,128]{4,3,2,1,0:T(8,128)S(1)}, u32[]{:S(2)}, u32[]{:S(2)}) %all-to-all-start.4) | async-done | bytes 786464 | tf_op jit(solution)/shard_map/all_to_all | solution.py:813
  282.8 4.2 %row_lines.7 = f32[8,2,3,32,128]{4,3,2,1,0:T(8,128)} custom-call(s32[5]{0:T(128)} %get-tuple-element.41.refs_0_.places, f32[8,2,3,32,128]{4,3,2,1,0:T(8,128)} %copy-done.13, f32[8,256]{1,0:T(8,128)} %constant.44.clone.refs_2_, bf16[512,512]{1,0:T(8,128)(2,1)} %constant.45.clone.refs_3_, bf16[512,512]{1,0:T(8,128)(2,1)} %constant.46.clone.refs_4_, ...), custom_call_target="tpu_custom_call" | custom-call | tf_op jit(solution)/shard_map/row_lines/pallas_call | solution.py:731
  286.9 3.5 %all-to-all-start.7 = ((f32[8,2,3,32,128]{4,3,2,1,0:T(8,128)}), f32[8,2,3,32,128]{4,3,2,1,0:T(8,128)S(1)}, u32[]{:S(2)}, u32[]{:S(2)}) async-start(f32[8,2,3,32,128]{4,3,2,1,0:T(8,128)} %row_lines.7), calls=%async_computation.7 | async-start | bytes 1572864 | tf_op jit(solution)/shard_map/all_to_all | solution.py:813
  290.5 2.0 collective-permute-start.8
  292.5 2.8 collective-permute-start.9
  296.5 12.6 %collective-permute-done.8.refs_9_ = f32[1,16,512]{2,1,0:T(8,128)S(1)} collective-permute-done((f32[1,16,512]{2,1,0:T(8,128)S(1)}, f32[1,16,512]{2,1,0:T(8,128)S(1)}, u32[]{:S(2)}, u32[]{:S(2)}) %collective-permute-start.8) | collective-permute-done | bytes 32800 | tf_op jit(solution)/shard_map/ppermute | solution.py:792
  309.7 11.8 %stencil.6.refs_0_.pre = f32[1,16,128,512]{3,2,1,0:T(8,128)} custom-call(s32[5]{0:T(128)} %get-tuple-element.41.refs_0_.places, f32[1,16,128,512]{3,2,1,0:T(8,128)} %get-tuple-element.25.refs_1_.refs_2_.refs_3_.refs_4_.phi, f32[1,16,128,512]{3,2,1,0:T(8,128)} %get-tuple-element.25.refs_1_.refs_2_.refs_3_.refs_4_.phi, ...), custom_call_target="tpu_custom_call" | custom-call | tf_op jit(solution)/shard_map/stencil/pallas_call | solution.py:367
  322.5 3.1 inverse_columns.7.refs_2_
  325.6 2.5 collective-permute-done.17.refs_3_
  329.0 8.1 %drive.3 = (f32[2,16,128,512]{3,2,1,0:T(8,128)}, f32[2,3,128,512]{3,2,1,0:T(8,128)}) custom-call(s32[5]{0:T(128)} %get-tuple-element.41.refs_0_.places, f32[1,16,128,512]{3,2,1,0:T(8,128)} %stencil.6.refs_0_.pre, f32[1,16,128,512]{3,2,1,0:T(8,128)} %get-tuple-element.25.refs_1_.refs_2_.refs_3_.refs_4_.phi, ...), custom_call_target="tpu_custom_call", output_to_operand_aliasing={{0}: (13, {}), {1}: (14, {})} | custom-call | tf_op jit(solution)/shard_map/drive/pallas_call | solution.py:487
  (91 shorter events, 22.1 us)
Async XLA Ops:
  2.0 16.0 %copy-start.22 = (f32[16,3]{0,1:T(4,128)S(1)}, f32[16,3]{0,1:T(4,128)}, u32[]{:S(2)}) copy-start(f32[16,3]{0,1:T(4,128)} %param.17) | copy-start | bytes 580
  8.0 11.3 %collective-permute-start = (f32[2,17,512]{2,1,0:T(8,128)}, f32[2,17,512]{2,1,0:T(8,128)S(1)}, u32[]{:S(2)}, u32[]{:S(2)}) collective-permute-start(f32[2,17,512]{2,1,0:T(8,128)} %get-tuple-element.20), channel_id=1, source_target_pairs={{0,2},{2,4},{4,6},{6,8},{8,10},{10,12},{12,14},{14,0},{1,3},{3,5},... | collective-permute-start | bytes 208904 | tf_op jit(solution)/shard_map/ppermute | solution.py:792
  11.0 8.3 %collective-permute-start.1 = (f32[2,17,512]{2,1,0:T(8,128)}, f32[2,17,512]{2,1,0:T(8,128)S(1)}, u32[]{:S(2)}, u32[]{:S(2)}) collective-permute-start(f32[2,17,512]{2,1,0:T(8,128)} %get-tuple-element.21), channel_id=1, source_target_pairs={{2,0},{4,2},{6,4},{8,6},{10,8},{12,10},{14,12},{0,14},{3,1},{5,3},... | collective-permute-start | bytes 208904 | tf_op jit(solution)/shard_map/ppermute | solution.py:793
  14.1 5.2 %collective-permute-start.2 = (f32[2,128,34]{2,1,0:T(8,128)}, f32[2,128,34]{2,1,0:T(8,128)S(1)}, u32[]{:S(2)}, u32[]{:S(2)}) collective-permute-start(f32[2,128,34]{2,1,0:T(8,128)} %get-tuple-element.22), channel_id=1, source_target_pairs={{0,1},{1,0},{2,3},{3,2},{4,5},{5,4},{6,7},{7,6},{8,9},{9,8},{10,11... | collective-permute-start | bytes 104456 | tf_op jit(solution)/shard_map/ppermute | solution.py:779
  14.2 25.2 %collective-permute-start.4 = (f32[2,2,128,512]{3,2,1,0:T(8,128)}, f32[2,2,128,512]{3,2,1,0:T(8,128)S(1)}, u32[]{:S(2)}, u32[]{:S(2)}) collective-permute-start(f32[2,2,128,512]{3,2,1,0:T(8,128)} %get-tuple-element.23.refs_3_.stiff), channel_id=1, source_target_pairs={{0,1},{1,0},{2,3},{3,2},{4,5},{5,4},{6,7},{7,6},{8,9},{9,8},{10,11... | collective-permute-start | bytes 3145736 | tf_op jit(solution)/shard_map/ppermute | solution.py:779
  19.3 0.7 copy-start.2
  19.4 0.7 copy-start.3
  32.1 7.3 %collective-permute-start.5 = (f32[3,128,512]{2,1,0:T(8,128)}, f32[3,128,512]{2,1,0:T(8,128)S(1)}, u32[]{:S(2)}, u32[]{:S(2)}) collective-permute-start(f32[3,128,512]{2,1,0:T(8,128)} %get-tuple-element.24.refs_5_.eigen), channel_id=1, source_target_pairs={{0,1},{1,0},{2,3},{3,2},{4,5},{5,4},{6,7},{7,6},{8,9},{9,8},{10,11... | collective-permute-start | bytes 2359304 | tf_op jit(solution)/shard_map/ppermute | solution.py:779
  37.0 93.3 %collective-permute-start.3 = (f32[1,16,128,512]{3,2,1,0:T(8,128)}, f32[1,16,128,512]{3,2,1,0:T(8,128)}, u32[]{:S(2)}, u32[]{:S(2)}) collective-permute-start(f32[1,16,128,512]{3,2,1,0:T(8,128)} %constant_dynamic-slice_fusion), channel_id=1, source_target_pairs={{0,16},{16,0},{1,17},{17,1},{2,18},{18,2},{3,19},{19,3},{4,20},{20... | collective-permute-start | bytes 12582920 | tf_op jit(solution)/shard_map/ppermute | solution.py:782
  39.3 0.9 copy-start.10
  39.3 1.2 copy-start
  45.2 24.3 %all-to-all-start = ((f32[8,2,3,32,128]{4,3,2,1,0:T(8,128)}), f32[8,2,3,32,128]{4,3,2,1,0:T(8,128)S(1)}, u32[]{:S(2)}, u32[]{:S(2)}) async-start(f32[8,2,3,32,128]{4,3,2,1,0:T(8,128)} %forward_columns.4), calls=%async_computation | async-start | bytes 1572864 | tf_op jit(solution)/shard_map/all_to_all | solution.py:813
  69.5 0.9 copy-start.12
  101.8 2.5 collective-permute-start.6
  104.3 0.9 copy-start.8
  137.7 36.8 %copy-start.28 = (f32[1,16,512]{2,1,0:T(8,128)S(1)}, f32[1,16,512]{2,1,0:T(8,128)}, u32[]{:S(2)}) copy-start(f32[1,16,512]{2,1,0:T(8,128)} %get-tuple-element.31) | copy-start | bytes 98308
  137.7 38.7 %copy-start.27 = (f32[1,16,512]{2,1,0:T(8,128)S(1)}, f32[1,16,512]{2,1,0:T(8,128)}, u32[]{:S(2)}) copy-start(f32[1,16,512]{2,1,0:T(8,128)} %get-tuple-element.32) | copy-start | bytes 98308
  137.7 41.5 %copy-start.24 = (f32[1,128,32]{2,1,0:T(8,128)S(1)}, f32[1,128,32]{2,1,0:T(8,128)}, u32[]{:S(2)}) copy-start(f32[1,128,32]{2,1,0:T(8,128)} %get-tuple-element.33) | copy-start | bytes 49156
  137.7 2.6 collective-permute-start.11
  140.3 0.9 copy-start.9
  170.7 37.8 %all-to-all-start.5 = ((f32[8,2,3,32,128]{4,3,2,1,0:T(8,128)}), f32[8,2,3,32,128]{4,3,2,1,0:T(8,128)S(1)}, u32[]{:S(2)}, u32[]{:S(2)}) async-start(f32[8,2,3,32,128]{4,3,2,1,0:T(8,128)} %forward_columns.5.refs_5_), calls=%async_computation.5 | async-start | bytes 1572864 | tf_op jit(solution)/shard_map/all_to_all | solution.py:813
  174.4 18.5 %collective-permute-start.12 = (f32[1,16,512]{2,1,0:T(8,128)S(1)}, f32[1,16,512]{2,1,0:T(8,128)S(1)}, u32[]{:S(2)}, u32[]{:S(2)}) collective-permute-start(f32[1,16,512]{2,1,0:T(8,128)S(1)} %copy-done.28), channel_id=1, source_target_pairs={{0,2},{2,4},{4,6},{6,8},{8,10},{10,12},{12,14},{14,0},{1,3},{3,5},... | collective-permute-start | bytes 98312 | tf_op jit(solution)/shard_map/ppermute | solution.py:792
  176.4 16.6 %collective-permute-start.13 = (f32[1,16,512]{2,1,0:T(8,128)S(1)}, f32[1,16,512]{2,1,0:T(8,128)S(1)}, u32[]{:S(2)}, u32[]{:S(2)}) collective-permute-start(f32[1,16,512]{2,1,0:T(8,128)S(1)} %copy-done.27), channel_id=1, source_target_pairs={{2,0},{4,2},{6,4},{8,6},{10,8},{12,10},{14,12},{0,14},{3,1},{5,3},... | collective-permute-start | bytes 98312 | tf_op jit(solution)/shard_map/ppermute | solution.py:793
  179.2 1.3 collective-permute-start.14
  180.5 12.4 %copy-start.17 = (f32[1,128,32]{2,1,0:T(8,128)}, f32[1,128,32]{2,1,0:T(8,128)S(1)}, u32[]{:S(2)}) copy-start(f32[1,128,32]{2,1,0:T(8,128)S(1)} %collective-permute-done.14.refs_10_) | copy-start | bytes 49156
  208.5 6.8 %copy-start.5 = (f32[8,2,3,32,128]{4,3,2,1,0:T(8,128)}, f32[8,2,3,32,128]{4,3,2,1,0:T(8,128)S(1)}, u32[]{:S(2)}) copy-start(f32[8,2,3,32,128]{4,3,2,1,0:T(8,128)S(1)} %all-to-all-done.5.refs_1_) | copy-start | bytes 2359300
  208.5 25.5 %all-to-all-start.3 = ((f32[8,2,3,32,128]{4,3,2,1,0:T(8,128)}), f32[8,2,3,32,128]{4,3,2,1,0:T(8,128)S(1)}, u32[]{:S(2)}, u32[]{:S(2)}) async-start(f32[8,2,3,32,128]{4,3,2,1,0:T(8,128)} %row_lines.5), calls=%async_computation.3 | async-start | bytes 1572864 | tf_op jit(solution)/shard_map/all_to_all | solution.py:813
  213.7 95.4 %collective-permute-start.7 = (f32[1,16,128,512]{3,2,1,0:T(8,128)}, f32[1,16,128,512]{3,2,1,0:T(8,128)}, u32[]{:S(2)}, u32[]{:S(2)}) collective-permute-start(f32[1,16,128,512]{3,2,1,0:T(8,128)} %get-tuple-element.25.refs_1_.refs_2_.refs_3_.refs_4_.phi), channel_id=1, source_target_pairs={{0,16},{16,0},{1,17},{17,1},{2,18},{18,2},{3,19},{19,3},{4,20},{20... | collective-permute-start | bytes 12582920 | tf_op jit(solution)/shard_map/ppermute | solution.py:782
  234.0 3.6 %copy-start.7 = (f32[8,2,3,32,128]{4,3,2,1,0:T(8,128)}, f32[8,2,3,32,128]{4,3,2,1,0:T(8,128)S(1)}, u32[]{:S(2)}) copy-start(f32[8,2,3,32,128]{4,3,2,1,0:T(8,128)S(1)} %all-to-all-done.3.recv) | copy-start | bytes 2359300
  234.0 23.9 %all-to-all-start.6 = ((f32[8,2,3,32,128]{4,3,2,1,0:T(8,128)}), f32[8,2,3,32,128]{4,3,2,1,0:T(8,128)S(1)}, u32[]{:S(2)}, u32[]{:S(2)}) async-start(f32[8,2,3,32,128]{4,3,2,1,0:T(8,128)} %row_lines.6), calls=%async_computation.6 | async-start | bytes 1572864 | tf_op jit(solution)/shard_map/all_to_all | solution.py:813
  240.7 2.5 collective-permute-start.15
  243.2 0.9 copy-start.4
  257.9 3.6 %copy-start.6 = (f32[8,2,3,32,128]{4,3,2,1,0:T(8,128)}, f32[8,2,3,32,128]{4,3,2,1,0:T(8,128)S(1)}, u32[]{:S(2)}) copy-start(f32[8,2,3,32,128]{4,3,2,1,0:T(8,128)S(1)} %all-to-all-done.6.recv) | copy-start | bytes 2359300
  257.9 23.9 %all-to-all-start.4 = ((f32[8,2,3,32,128]{4,3,2,1,0:T(8,128)}), f32[8,2,3,32,128]{4,3,2,1,0:T(8,128)S(1)}, u32[]{:S(2)}, u32[]{:S(2)}) async-start(f32[8,2,3,32,128]{4,3,2,1,0:T(8,128)} %forward_columns.7), calls=%async_computation.4 | async-start | bytes 1572864 | tf_op jit(solution)/shard_map/all_to_all | solution.py:813
  264.7 2.5 collective-permute-start.16
  267.1 0.9 copy-start.15
  281.9 0.9 copy-start.13
  282.8 7.7 %copy-start.26 = (f32[1,16,512]{2,1,0:T(8,128)S(1)}, f32[1,16,512]{2,1,0:T(8,128)}, u32[]{:S(2)}) copy-start(f32[1,16,512]{2,1,0:T(8,128)} %get-tuple-element.27) | copy-start | bytes 98308
  282.8 9.7 %copy-start.25 = (f32[1,16,512]{2,1,0:T(8,128)S(1)}, f32[1,16,512]{2,1,0:T(8,128)}, u32[]{:S(2)}) copy-start(f32[1,16,512]{2,1,0:T(8,128)} %get-tuple-element.28) | copy-start | bytes 98308
  282.8 12.5 %copy-start.23 = (f32[1,128,32]{2,1,0:T(8,128)S(1)}, f32[1,128,32]{2,1,0:T(8,128)}, u32[]{:S(2)}) copy-start(f32[1,128,32]{2,1,0:T(8,128)} %get-tuple-element.29) | copy-start | bytes 49156
  286.9 34.6 %all-to-all-start.7 = ((f32[8,2,3,32,128]{4,3,2,1,0:T(8,128)}), f32[8,2,3,32,128]{4,3,2,1,0:T(8,128)S(1)}, u32[]{:S(2)}, u32[]{:S(2)}) async-start(f32[8,2,3,32,128]{4,3,2,1,0:T(8,128)} %row_lines.7), calls=%async_computation.7 | async-start | bytes 1572864 | tf_op jit(solution)/shard_map/all_to_all | solution.py:813
  290.5 18.6 %collective-permute-start.8 = (f32[1,16,512]{2,1,0:T(8,128)S(1)}, f32[1,16,512]{2,1,0:T(8,128)S(1)}, u32[]{:S(2)}, u32[]{:S(2)}) collective-permute-start(f32[1,16,512]{2,1,0:T(8,128)S(1)} %copy-done.26), channel_id=1, source_target_pairs={{0,2},{2,4},{4,6},{6,8},{8,10},{10,12},{12,14},{14,0},{1,3},{3,5},... | collective-permute-start | bytes 98312 | tf_op jit(solution)/shard_map/ppermute | solution.py:792
  292.5 16.6 %collective-permute-start.9 = (f32[1,16,512]{2,1,0:T(8,128)S(1)}, f32[1,16,512]{2,1,0:T(8,128)S(1)}, u32[]{:S(2)}, u32[]{:S(2)}) collective-permute-start(f32[1,16,512]{2,1,0:T(8,128)S(1)} %copy-done.25), channel_id=1, source_target_pairs={{2,0},{4,2},{6,4},{8,6},{10,8},{12,10},{14,12},{0,14},{3,1},{5,3},... | collective-permute-start | bytes 98312 | tf_op jit(solution)/shard_map/ppermute | solution.py:793
  295.3 1.3 collective-permute-start.10
  296.5 12.6 %copy-start.16 = (f32[1,128,32]{2,1,0:T(8,128)}, f32[1,128,32]{2,1,0:T(8,128)S(1)}, u32[]{:S(2)}) copy-start(f32[1,128,32]{2,1,0:T(8,128)S(1)} %collective-permute-done.10.refs_11_) | copy-start | bytes 49156
  321.5 0.9 copy-start.11
  325.6 2.5 collective-permute-start.17
  328.1 0.9 copy-start.14
  (5 other events, 3.1 us)
where the time goes:
time: 339 us; the launch traced here: 337 us
  Pallas kernels  124 us (37%)
  waiting for transfers between devices  97.7 us (29%)
  blocking collectives  49 us (14%)
  starting transfers between devices  42.8 us (13%)
  local copies, waits for them, and re-layouts  18.5 us (5%)
  other arithmetic  3.95 us (1%)
    all_to_all x2, blocking collectives, exchange(): return lax.all_to_all(value, 'row', split_axis=0, concat_axis=0, tiled=True)  49 us
    pallas_call x4, Pallas kernels, run_stencil(): pl.pallas_call(kernel, grid_spec=pltpu.PrefetchScalarGridSpec(num_scalar_...  45.4 us
    all_to_all x6, waiting for transfers between devices, exchange(): return lax.all_to_all(value, 'row', split_axis=0, concat_axis=0, tiled=True)  38 us
    ppermute x3, waiting for transfers between devices, move_edges(): lax.ppermute(bottom, 'row', ring_up)  25 us
    all_to_all x6, starting transfers between devices, exchange(): return lax.all_to_all(value, 'row', split_axis=0, concat_axis=0, tiled=True)  23.1 us
    pallas_call x4, Pallas kernels, run_forward(): pl.pallas_call(kernel, grid_spec=pltpu.PrefetchScalarGridSpec(num_scalar_...  19.9 us
    ppermute x2, waiting for transfers between devices, swap_layers(): return lax.ppermute(value, 'grp', swap_pairs)  19.7 us
    pallas_call x4, Pallas kernels, run_rows(): pl.pallas_call(kernel, in_specs=[pl.BlockSpec(memory_space=pltpu.SMEM), w...  16.6 us
  transfers between devices with their start and end apart: 24, of which 14 were waited for; matrix products, arithmetic and copies ran while one was open for 3% of the time, Pallas kernels for 28%

commit v1 on v0

--- a/solution.py
+++ b/solution.py
@@ -21,6 +21,7 @@
 LANES = 128
 RADIX = 4
 VMEM_LIMIT = 56 * 1024 * 1024
+VMEM_SMALL = 16 * 1024 * 1024
 
 
 def split3(value):
@@ -71,9 +72,10 @@
 
 
 def prepare_kernel(
-    grain, phase, top_rows, bottom_rows, left, right, speeds, index, table,
-    mobility, stiff, edge_up, edge_dn, edge_col,
+    which, grain, phase, top_rows, bottom_rows, left, right, whole, speeds, index, table,
+    mobility, stiff, edge_up, edge_dn, edge_col, layer,
 ):
+    layer[...] = whole[...]
     count, rows = left.shape[1], left.shape[2]
     width = left.shape[3]
     labels = grain[0]
@@ -111,32 +113,41 @@
         edge_dn[0, count : count + 1, :] = speed[rows - 1 : rows, :]
 
 
-def run_prepare(order_field, grain_label, phase_label, grain_mobility, stiff_index, stiff_table):
+def run_prepare(
+    order_field, grain_label, phase_label, grain_mobility, stiff_index, stiff_table, which
+):
     layers, count, rows, cols = order_field.shape
     block = min(rows, 8 * STRIP)
     width = min(cols, LANES)
+    steps = rows // block
+    piece = rows // (layers * steps)
     smem = pl.BlockSpec(memory_space=pltpu.SMEM)
     shape = jax.ShapeDtypeStruct
     return pl.pallas_call(
         prepare_kernel,
-        grid=(layers, rows // block),
+        grid_spec=pltpu.PrefetchScalarGridSpec(
+        num_scalar_prefetch=1,
+        grid=(layers, steps),
         in_specs=[
-            pl.BlockSpec((1, block, cols), lambda l, r: (l, r, 0)),
-            pl.BlockSpec((1, block, cols), lambda l, r: (l, r, 0)),
-            pl.BlockSpec((1, count, STRIP, cols), lambda l, r: (l, 0, 0, 0)),
-            pl.BlockSpec((1, count, STRIP, cols), lambda l, r: (l, 0, rows // STRIP - 1, 0)),
-            pl.BlockSpec((1, count, block, width), lambda l, r: (l, 0, r, 0)),
-            pl.BlockSpec((1, count, block, width), lambda l, r: (l, 0, r, cols // width - 1)),
+            pl.BlockSpec((1, block, cols), lambda l, r, w: (l, r, 0)),
+            pl.BlockSpec((1, block, cols), lambda l, r, w: (l, r, 0)),
+            pl.BlockSpec((1, count, STRIP, cols), lambda l, r, w: (l, 0, 0, 0)),
+            pl.BlockSpec((1, count, STRIP, cols), lambda l, r, w: (l, 0, rows // STRIP - 1, 0)),
+            pl.BlockSpec((1, count, block, width), lambda l, r, w: (l, 0, r, 0)),
+            pl.BlockSpec((1, count, block, width), lambda l, r, w: (l, 0, r, cols // width - 1)),
+            pl.BlockSpec((1, count, piece, cols), lambda l, r, w: (w[0], 0, l * steps + r, 0)),
             smem,
             smem,
             smem,
         ],
         out_specs=(
-            pl.BlockSpec((1, block, cols), lambda l, r: (l, r, 0)),
-            pl.BlockSpec((1, 2, block, cols), lambda l, r: (l, 0, r, 0)),
-            pl.BlockSpec((1, count + 1, cols), lambda l, r: (l, 0, 0)),
-            pl.BlockSpec((1, count + 1, cols), lambda l, r: (l, 0, 0)),
-            pl.BlockSpec((1, block, 2 * count + 2), lambda l, r: (l, r, 0)),
+            pl.BlockSpec((1, block, cols), lambda l, r, w: (l, r, 0)),
+            pl.BlockSpec((1, 2, block, cols), lambda l, r, w: (l, 0, r, 0)),
+            pl.BlockSpec((1, count + 1, cols), lambda l, r, w: (l, 0, 0)),
+            pl.BlockSpec((1, count + 1, cols), lambda l, r, w: (l, 0, 0)),
+            pl.BlockSpec((1, block, 2 * count + 2), lambda l, r, w: (l, r, 0)),
+            pl.BlockSpec((1, count, piece, cols), lambda l, r, w: (0, 0, l * steps + r, 0)),
+        ),
         ),
         out_shape=(
             shape((layers, rows, cols), jnp.float32),
@@ -144,12 +155,13 @@
             shape((layers, count + 1, cols), jnp.float32),
             shape((layers, count + 1, cols), jnp.float32),
             shape((layers, rows, 2 * count + 2), jnp.float32),
+            shape((1, count, rows, cols), jnp.float32),
         ),
         compiler_params=pltpu.CompilerParams(vmem_limit_bytes=VMEM_LIMIT),
         name="prepare",
     )(
-        grain_label, phase_label, order_field, order_field, order_field, order_field,
-        grain_mobility, stiff_index, stiff_table,
+        which, grain_label, phase_label, order_field, order_field, order_field, order_field,
+        order_field, grain_mobility, stiff_index, stiff_table,
     )
 
 
@@ -399,7 +411,7 @@
 def run_finish(places, partial, remote, mobility, eigen_strain, after):
     _, rows, cols = mobility.shape
     count = partial.shape[1]
-    block = min(rows, 4 * STRIP)
+    block = min(rows, 2 * STRIP)
     field = pl.BlockSpec((1, count, block, cols), lambda r, p: (0, 0, r, 0))
     out_shape, out_specs = rim_outputs(count, rows, cols, block)
 
@@ -461,7 +473,7 @@
 def run_drive(places, pre, fields, mobility, stiff, eigen, eigen_strain, signs, macro, swaps, held):
     layers, rows, cols = mobility.shape
     count = fields.shape[1]
-    block = min(rows, 4 * STRIP)
+    block = min(rows, 2 * STRIP)
     smem = pl.BlockSpec(memory_space=pltpu.SMEM)
     field = pl.BlockSpec((1, count, block, cols), lambda r, p: (0, 0, r, 0))
     plane = pl.BlockSpec((3, block, cols), lambda r, p: (0, r, 0))
@@ -610,7 +622,7 @@
         out_specs=whole,
         out_shape=jax.ShapeDtypeStruct((3, rows, cols), jnp.float32),
         scratch_shapes=[pltpu.VMEM((width, 3 * rows), jnp.float32)],
-        compiler_params=pltpu.CompilerParams(vmem_limit_bytes=VMEM_LIMIT),
+        compiler_params=pltpu.CompilerParams(vmem_limit_bytes=VMEM_SMALL),
         name="inverse_columns",
     )(recv, *waves, *after)
 
@@ -734,7 +746,7 @@
         out_specs=whole,
         out_shape=jax.ShapeDtypeStruct(recv.shape, jnp.float32),
         scratch_shapes=[pltpu.VMEM((RADIX * 3 * part, 2 * span), jnp.float32)],
-        compiler_params=pltpu.CompilerParams(vmem_limit_bytes=VMEM_LIMIT),
+        compiler_params=pltpu.CompilerParams(vmem_limit_bytes=VMEM_SMALL),
         name="row_lines",
     )(places, recv, *tables, *after)
     if not dense:
@@ -781,11 +793,16 @@
     def swap_layers(value):
         return lax.ppermute(value, "grp", swap_pairs)
 
-    remote_field = swap_layers(lax.dynamic_slice_in_dim(order_field, outer, 1, 0))
-
-    mobility, stiff, top, bottom, sides = run_prepare(
-        order_field, grain_label, phase_label, grain_mobility, stiff_index, stiff_table
-    )
+    mobility, stiff, top, bottom, sides, edge_layer = run_prepare(
+        order_field,
+        grain_label,
+        phase_label,
+        grain_mobility,
+        stiff_index,
+        stiff_table,
+        outer[None],
+    )
+    remote_field = swap_layers(edge_layer)
 
     def move_edges(top, bottom, sides):
         return (

time: 339 us -> 344 us (1.015)
  Pallas kernels: 124 us -> 118 us
  local copies, waits for them, and re-layouts: 18.5 us -> 24.4 us
  waiting for transfers between devices: 97.7 us -> 102 us
    unnamed x60 -> x96, local copies, waits for them, and re-layouts: 11.8 us -> 22.3 us
    pallas_call x4, Pallas kernels: 12.6 us -> 5.48 us  [run_inverse(): pl.pallas_call(inverse_kernel, in_specs=[whole, whole, whole, *any_specs(...]
    pallas_call x4, Pallas kernels: 16.6 us -> 10.2 us  [run_rows(): pl.pallas_call(kernel, in_specs=[pl.BlockSpec(memory_space=pltpu.SMEM), w...]
    dynamic_slice x1 -> x0, local copies, waits for them, and re-layouts: 4.8 us -> none  [body(): lax.dynamic_slice_in_dim(order_field, outer, 1, 0)]
    pallas_call x2, Pallas kernels: 16.2 us -> 19.7 us  [run_drive(): pl.pallas_call(drive_kernel, grid_spec=pltpu.PrefetchScalarGridSpec(num_s...]
  transfers between devices with their start and end apart: 24 -> 24, of which waited for: 14 -> 14; matrix products, arithmetic and copies ran while one was open for 3% -> 2% of each run, Pallas kernels for 28% -> 25%
where the time goes in v1:
time: 344 us; the launch traced here: 341 us
  Pallas kernels  118 us (34%)
  waiting for transfers between devices  102 us (30%)
  blocking collectives  47.9 us (14%)
  starting transfers between devices  44.2 us (13%)
  local copies, waits for them, and re-layouts  24.4 us (7%)
  other arithmetic  3.97 us (1%)
    all_to_all x2, blocking collectives, exchange(): return lax.all_to_all(value, 'row', split_axis=0, concat_axis=0, tiled=True)  47.9 us
    pallas_call x4, Pallas kernels, run_stencil(): pl.pallas_call(kernel, grid_spec=pltpu.PrefetchScalarGridSpec(num_scalar_...  45.5 us
    all_to_all x6, waiting for transfers between devices, exchange(): return lax.all_to_all(value, 'row', split_axis=0, concat_axis=0, tiled=True)  39.5 us
    ppermute x3, waiting for transfers between devices, move_edges(): lax.ppermute(bottom, 'row', ring_up)  24.9 us
    all_to_all x6, starting transfers between devices, exchange(): return lax.all_to_all(value, 'row', split_axis=0, concat_axis=0, tiled=True)  23.8 us
    ppermute x2, waiting for transfers between devices, swap_layers(): return lax.ppermute(value, 'grp', swap_pairs)  23.1 us
    unnamed x96, local copies, waits for them, and re-layouts  22.3 us
    pallas_call x4, Pallas kernels, run_forward(): pl.pallas_call(kernel, grid_spec=pltpu.PrefetchScalarGridSpec(num_scalar_...  19.9 us
  transfers between devices with their start and end apart: 24, of which 14 were waited for; matrix products, arithmetic and copies ran while one was open for 2% of the time, Pallas kernels for 25%

profile of v1, /device:TPU:0, one launch (start us, length us, event | category | flops | bytes accessed | tf_op | source)
XLA Modules:
  0.0 341.4 jit_solution(12352061588842350420)
XLA Ops:
  2.0 8.0 %prepare.1 = (f32[2,128,512]{2,1,0:T(8,128)}, f32[2,2,128,512]{3,2,1,0:T(8,128)}, f32[2,17,512]{2,1,0:T(8,128)}, f32[2,17,512]{2,1,0:T(8,128)}, f32[2,128,34]{2,1,0:T(8,128)}, /*index=5*/f32[1,16,128,512]{3,2,1,0:T(8,128)}) custom-call(s32[1]{0:T(128)} %bitcast.which, s32[2,128,512]{2,1,0:T(8,128)} %grain.1, s32[2,128,512]{2,1,0:T(8,128)} %phase.1, ...), custom_call_target="tpu_custom_call" | custom-call | tf_op jit(solution)/shard_map/prepare/pallas_call | solution.py:126
  10.0 3.0 collective-permute-start
  13.0 3.1 collective-permute-start.1
  16.7 2.1 cosine_bitcast_fusion
  22.1 12.0 %stencil.5 = (f32[1,16,128,512]{3,2,1,0:T(8,128)}, f32[3,128,512]{2,1,0:T(8,128)}, f32[1,16,512]{2,1,0:T(8,128)}, f32[1,16,512]{2,1,0:T(8,128)}, f32[1,128,32]{2,1,0:T(8,128)}) custom-call(s32[5]{0:T(128)} %stack.23.refs_0_, f32[2,16,128,512]{3,2,1,0:T(8,128)} %refs_4_.7, f32[2,16,128,512]{3,2,1,0:T(8,128)} %refs_4_.7, f32[2,16,128,512]{3,2,1,0:T(8,128)} %refs_4_.7, ...), custom_call_target="tpu_custom_call" | custom-call | tf_op jit(solution)/shard_map/stencil/pallas_call | solution.py:379
  38.0 4.7 %forward_columns.4 = f32[8,2,3,32,128]{4,3,2,1,0:T(8,128)} custom-call(s32[5]{0:T(128)} %get-tuple-element.42.refs_0_.places, f32[1]{0:T(128)} %bitcast.4.refs_1_.signs, f32[3]{0:T(128)} %macro.3, f32[2,2,128,512]{3,2,1,0:T(8,128)} %get-tuple-element.25.refs_3_.stiff, f32[2,2,128,512]{3,2,1,0:T(8,128)} %copy-done.24, ...), custom_call_target="tpu_custom_call" | custom-call | tf_op jit(solution)/shard_map/forward_columns/pallas_call | solution.py:586
  42.6 3.5 %all-to-all-start = ((f32[8,2,3,32,128]{4,3,2,1,0:T(8,128)}), f32[8,2,3,32,128]{4,3,2,1,0:T(8,128)S(1)}, u32[]{:S(2)}, u32[]{:S(2)}) async-start(f32[8,2,3,32,128]{4,3,2,1,0:T(8,128)} %forward_columns.4), calls=%async_computation | async-start | bytes 1572864 | tf_op jit(solution)/shard_map/all_to_all | solution.py:830
  46.9 10.9 %stencil.4.refs_5_.refs_1_ = f32[1,16,128,512]{3,2,1,0:T(8,128)} custom-call(s32[5]{0:T(128)} %stack.21.refs_0_, f32[2,16,128,512]{3,2,1,0:T(8,128)} %refs_4_.7, f32[2,16,128,512]{3,2,1,0:T(8,128)} %refs_4_.7, f32[2,16,128,512]{3,2,1,0:T(8,128)} %refs_4_.7, f32[2,16,128,512]{3,2,1,0:T(8,128)} %refs_4_.7, ...), custom_call_target="tpu_custom_call" | custom-call | tf_op jit(solution)/shard_map/stencil/pallas_call | solution.py:379
  57.8 9.0 %all-to-all-done.refs_1_ = f32[8,2,3,32,128]{4,3,2,1,0:T(8,128)S(1)} async-done(((f32[8,2,3,32,128]{4,3,2,1,0:T(8,128)}), f32[8,2,3,32,128]{4,3,2,1,0:T(8,128)S(1)}, u32[]{:S(2)}, u32[]{:S(2)}) %all-to-all-start) | async-done | bytes 786464 | tf_op jit(solution)/shard_map/all_to_all | solution.py:830
  66.9 2.2 copy-done.6
  69.1 2.3 row_lines.4
  71.4 23.7 %all_to_all.40.recv = f32[8,2,3,32,128]{4,3,2,1,0:T(8,128)S(1)} all-to-all(f32[8,2,3,32,128]{4,3,2,1,0:T(8,128)S(1)} %row_lines.4), channel_id=1, replica_groups=mesh['grp'=2,'row'=8,'col'=2] {'row'}, dimensions={0} | all-to-all | bytes 1572864 | tf_op jit(solution)/shard_map/all_to_all | solution.py:830
  96.0 2.3 collective-permute-done.6.refs_8_.refs_1_
  99.2 5.3 %forward_columns.5.refs_5_ = f32[8,2,3,32,128]{4,3,2,1,0:T(8,128)} custom-call(s32[5]{0:T(128)} %get-tuple-element.42.refs_0_.places, f32[1]{0:T(128)} %bitcast.4.refs_1_.signs, f32[3]{0:T(128)} %macro.3, f32[2,2,128,512]{3,2,1,0:T(8,128)} %get-tuple-element.25.refs_3_.stiff, f32[2,2,128,512]{3,2,1,0:T(8,128)} %copy-done.24, ...), custom_call_target="tpu_custom_call" | custom-call | tf_op jit(solution)/shard_map/forward_columns/pallas_call | solution.py:586
  104.5 23.1 %collective-permute-done.3.refs_2_ = f32[1,16,128,512]{3,2,1,0:T(8,128)} collective-permute-done((f32[1,16,128,512]{3,2,1,0:T(8,128)}, f32[1,16,128,512]{3,2,1,0:T(8,128)}, u32[]{:S(2)}, u32[]{:S(2)}) %collective-permute-start.3) | collective-permute-done | bytes 4194336 | tf_op jit(solution)/shard_map/ppermute | solution.py:794
  127.5 9.3 %finish.1 = (f32[1,16,128,512]{3,2,1,0:T(8,128)}, f32[3,128,512]{2,1,0:T(8,128)}, f32[1,16,512]{2,1,0:T(8,128)}, f32[1,16,512]{2,1,0:T(8,128)}, f32[1,128,32]{2,1,0:T(8,128)}) custom-call(s32[5]{0:T(128)} %get-tuple-element.43.refs_0_.places, f32[1,16,128,512]{3,2,1,0:T(8,128)} %stencil.4.refs_5_.refs_1_, ...), custom_call_target="tpu_custom_call" | custom-call | tf_op jit(solution)/shard_map/finish/pallas_call | solution.py:421
  137.0 2.5 collective-permute-done.11.refs_6_
  140.4 4.7 %forward_columns.6 = f32[8,2,3,32,128]{4,3,2,1,0:T(8,128)} custom-call(s32[5]{0:T(128)} %get-tuple-element.43.refs_0_.places, f32[1]{0:T(128)} %bitcast.4.refs_1_.signs, f32[3]{0:T(128)} %macro.3, f32[2,2,128,512]{3,2,1,0:T(8,128)} %get-tuple-element.25.refs_3_.stiff, f32[2,2,128,512]{3,2,1,0:T(8,128)} %copy-done.24, ...), custom_call_target="tpu_custom_call" | custom-call | tf_op jit(solution)/shard_map/forward_columns/pallas_call | solution.py:586
  145.0 24.1 %all_to_all.41.refs_1_ = f32[8,2,3,32,128]{4,3,2,1,0:T(8,128)S(1)} all-to-all(f32[8,2,3,32,128]{4,3,2,1,0:T(8,128)} %forward_columns.6), channel_id=1, replica_groups=mesh['grp'=2,'row'=8,'col'=2] {'row'}, dimensions={0} | all-to-all | bytes 1572864 | tf_op jit(solution)/shard_map/all_to_all | solution.py:830
  169.2 3.6 %all-to-all-start.5 = ((f32[8,2,3,32,128]{4,3,2,1,0:T(8,128)}), f32[8,2,3,32,128]{4,3,2,1,0:T(8,128)S(1)}, u32[]{:S(2)}, u32[]{:S(2)}) async-start(f32[8,2,3,32,128]{4,3,2,1,0:T(8,128)} %forward_columns.5.refs_5_), calls=%async_computation.5 | async-start | bytes 1572864 | tf_op jit(solution)/shard_map/all_to_all | solution.py:830
  172.8 2.0 collective-permute-start.12
  174.8 2.9 collective-permute-start.13
  179.0 12.4 %collective-permute-done.12.refs_8_ = f32[1,16,512]{2,1,0:T(8,128)S(1)} collective-permute-done((f32[1,16,512]{2,1,0:T(8,128)S(1)}, f32[1,16,512]{2,1,0:T(8,128)S(1)}, u32[]{:S(2)}, u32[]{:S(2)}) %collective-permute-start.12) | collective-permute-done | bytes 32800 | tf_op jit(solution)/shard_map/ppermute | solution.py:809
  192.0 10.9 %stencil.7.refs_5_.pre = f32[1,16,128,512]{3,2,1,0:T(8,128)} custom-call(s32[5]{0:T(128)} %get-tuple-element.42.refs_0_.places, f32[1,16,128,512]{3,2,1,0:T(8,128)} %get-tuple-element.28.refs_4_.refs_1_.refs_2_.refs_3_.phi, f32[1,16,128,512]{3,2,1,0:T(8,128)} %get-tuple-element.28.refs_4_.refs_1_.refs_2_.refs_3_.phi, ...), custom_call_target="tpu_custom_call" | custom-call | tf_op jit(solution)/shard_map/stencil/pallas_call | solution.py:379
  202.9 2.2 copy-done.7
  205.1 2.3 row_lines.5
  208.3 5.3 %all-to-all-start.3 = ((f32[8,2,3,32,128]{4,3,2,1,0:T(8,128)}), f32[8,2,3,32,128]{4,3,2,1,0:T(8,128)}, u32[]{:S(2)}, u32[]{:S(2)}) async-start(f32[8,2,3,32,128]{4,3,2,1,0:T(8,128)} %copy-done.18), calls=%async_computation.3 | async-start | bytes 1572864 | tf_op jit(solution)/shard_map/all_to_all | solution.py:830
  215.4 2.3 row_lines.6
  218.7 15.9 %all-to-all-done.3.recv = f32[8,2,3,32,128]{4,3,2,1,0:T(8,128)} async-done(((f32[8,2,3,32,128]{4,3,2,1,0:T(8,128)}), f32[8,2,3,32,128]{4,3,2,1,0:T(8,128)}, u32[]{:S(2)}, u32[]{:S(2)}) %all-to-all-start.3) | async-done | bytes 786464 | tf_op jit(solution)/shard_map/all_to_all | solution.py:830
  234.6 4.2 %all-to-all-start.6 = ((f32[8,2,3,32,128]{4,3,2,1,0:T(8,128)}), f32[8,2,3,32,128]{4,3,2,1,0:T(8,128)}, u32[]{:S(2)}, u32[]{:S(2)}) async-start(f32[8,2,3,32,128]{4,3,2,1,0:T(8,128)} %copy-done.17), calls=%async_computation.6 | async-start | bytes 1572864 | tf_op jit(solution)/shard_map/all_to_all | solution.py:830
  240.9 2.3 collective-permute-done.15.refs_8_.refs_1_
  244.1 5.3 %forward_columns.7 = f32[8,2,3,32,128]{4,3,2,1,0:T(8,128)} custom-call(s32[5]{0:T(128)} %get-tuple-element.43.refs_0_.places, f32[1]{0:T(128)} %bitcast.4.refs_1_.signs, f32[3]{0:T(128)} %macro.3, f32[2,2,128,512]{3,2,1,0:T(8,128)} %get-tuple-element.25.refs_3_.stiff, f32[2,2,128,512]{3,2,1,0:T(8,128)} %copy-done.24, ...), custom_call_target="tpu_custom_call" | custom-call | tf_op jit(solution)/shard_map/forward_columns/pallas_call | solution.py:586
  249.3 9.4 %all-to-all-done.6.recv = f32[8,2,3,32,128]{4,3,2,1,0:T(8,128)} async-done(((f32[8,2,3,32,128]{4,3,2,1,0:T(8,128)}), f32[8,2,3,32,128]{4,3,2,1,0:T(8,128)}, u32[]{:S(2)}, u32[]{:S(2)}) %all-to-all-start.6) | async-done | bytes 786464 | tf_op jit(solution)/shard_map/all_to_all | solution.py:830
  258.8 3.5 %all-to-all-start.4 = ((f32[8,2,3,32,128]{4,3,2,1,0:T(8,128)}), f32[8,2,3,32,128]{4,3,2,1,0:T(8,128)S(1)}, u32[]{:S(2)}, u32[]{:S(2)}) async-start(f32[8,2,3,32,128]{4,3,2,1,0:T(8,128)} %forward_columns.7), calls=%async_computation.4 | async-start | bytes 1572864 | tf_op jit(solution)/shard_map/all_to_all | solution.py:830
  262.3 1.9 inverse_columns.6.refs_2_
  264.4 2.3 collective-permute-done.16.refs_3_
  267.6 9.8 %drive.2 = (f32[2,16,128,512]{3,2,1,0:T(8,128)}, f32[2,3,128,512]{3,2,1,0:T(8,128)}) custom-call(s32[5]{0:T(128)} %get-tuple-element.42.refs_0_.places, f32[1,16,128,512]{3,2,1,0:T(8,128)} %stencil.7.refs_5_.pre, f32[1,16,128,512]{3,2,1,0:T(8,128)} %get-tuple-element.28.refs_4_.refs_1_.refs_2_.refs_3_.phi, ...), custom_call_target="tpu_custom_call" | custom-call | tf_op jit(solution)/shard_map/drive/pallas_call | solution.py:499
  277.5 5.1 %all-to-all-done.4.refs_1_ = f32[8,2,3,32,128]{4,3,2,1,0:T(8,128)S(1)} async-done(((f32[8,2,3,32,128]{4,3,2,1,0:T(8,128)}), f32[8,2,3,32,128]{4,3,2,1,0:T(8,128)S(1)}, u32[]{:S(2)}, u32[]{:S(2)}) %all-to-all-start.4) | async-done | bytes 786464 | tf_op jit(solution)/shard_map/all_to_all | solution.py:830
  282.6 3.4 copy-done.9
  287.4 3.2 row_lines.7
  290.6 3.6 %all-to-all-start.7 = ((f32[8,2,3,32,128]{4,3,2,1,0:T(8,128)}), f32[8,2,3,32,128]{4,3,2,1,0:T(8,128)S(1)}, u32[]{:S(2)}, u32[]{:S(2)}) async-start(f32[8,2,3,32,128]{4,3,2,1,0:T(8,128)} %row_lines.7), calls=%async_computation.7 | async-start | bytes 1572864 | tf_op jit(solution)/shard_map/all_to_all | solution.py:830
  294.2 2.0 collective-permute-start.8
  296.2 2.8 collective-permute-start.9
  300.2 12.6 %collective-permute-done.8.refs_9_ = f32[1,16,512]{2,1,0:T(8,128)S(1)} collective-permute-done((f32[1,16,512]{2,1,0:T(8,128)S(1)}, f32[1,16,512]{2,1,0:T(8,128)S(1)}, u32[]{:S(2)}, u32[]{:S(2)}) %collective-permute-start.8) | collective-permute-done | bytes 32800 | tf_op jit(solution)/shard_map/ppermute | solution.py:809
  313.4 11.7 %stencil.6.refs_0_.pre = f32[1,16,128,512]{3,2,1,0:T(8,128)} custom-call(s32[5]{0:T(128)} %get-tuple-element.43.refs_0_.places, f32[1,16,128,512]{3,2,1,0:T(8,128)} %get-tuple-element.27.refs_1_.refs_2_.refs_3_.refs_4_.phi, f32[1,16,128,512]{3,2,1,0:T(8,128)} %get-tuple-element.27.refs_1_.refs_2_.refs_3_.refs_4_.phi, ...), custom_call_target="tpu_custom_call" | custom-call | tf_op jit(solution)/shard_map/stencil/pallas_call | solution.py:379
  325.1 2.2 copy-done.8
  328.2 2.3 collective-permute-done.17.refs_3_
  331.4 9.8 %drive.3 = (f32[2,16,128,512]{3,2,1,0:T(8,128)}, f32[2,3,128,512]{3,2,1,0:T(8,128)}) custom-call(s32[5]{0:T(128)} %get-tuple-element.43.refs_0_.places, f32[1,16,128,512]{3,2,1,0:T(8,128)} %stencil.6.refs_0_.pre, f32[1,16,128,512]{3,2,1,0:T(8,128)} %get-tuple-element.27.refs_1_.refs_2_.refs_3_.refs_4_.phi, ...), custom_call_target="tpu_custom_call", output_to_operand_aliasing={{0}: (13, {}), {1}: (14, {})} | custom-call | tf_op jit(solution)/shard_map/drive/pallas_call | solution.py:499
  (126 shorter events, 26.8 us)
Async XLA Ops:
  2.0 18.0 %copy-start.40 = (f32[16,3]{0,1:T(4,128)S(1)}, f32[16,3]{0,1:T(4,128)}, u32[]{:S(2)}) copy-start(f32[16,3]{0,1:T(4,128)} %param.17) | copy-start | bytes 580
  10.0 11.4 %collective-permute-start = (f32[2,17,512]{2,1,0:T(8,128)}, f32[2,17,512]{2,1,0:T(8,128)S(1)}, u32[]{:S(2)}, u32[]{:S(2)}) collective-permute-start(f32[2,17,512]{2,1,0:T(8,128)} %get-tuple-element.21), channel_id=1, source_target_pairs={{0,2},{2,4},{4,6},{6,8},{8,10},{10,12},{12,14},{14,0},{1,3},{3,5},... | collective-permute-start | bytes 208904 | tf_op jit(solution)/shard_map/ppermute | solution.py:809
  13.0 8.4 %collective-permute-start.1 = (f32[2,17,512]{2,1,0:T(8,128)}, f32[2,17,512]{2,1,0:T(8,128)S(1)}, u32[]{:S(2)}, u32[]{:S(2)}) collective-permute-start(f32[2,17,512]{2,1,0:T(8,128)} %get-tuple-element.22), channel_id=1, source_target_pairs={{2,0},{4,2},{6,4},{8,6},{10,8},{12,10},{14,12},{0,14},{3,1},{5,3},... | collective-permute-start | bytes 208904 | tf_op jit(solution)/shard_map/ppermute | solution.py:810
  16.1 5.3 %collective-permute-start.2 = (f32[2,128,34]{2,1,0:T(8,128)}, f32[2,128,34]{2,1,0:T(8,128)S(1)}, u32[]{:S(2)}, u32[]{:S(2)}) collective-permute-start(f32[2,128,34]{2,1,0:T(8,128)} %get-tuple-element.23), channel_id=1, source_target_pairs={{0,1},{1,0},{2,3},{3,2},{4,5},{5,4},{6,7},{7,6},{8,9},{9,8},{10,11... | collective-permute-start | bytes 104456 | tf_op jit(solution)/shard_map/ppermute | solution.py:791
  16.2 20.6 %collective-permute-start.4 = (f32[2,2,128,512]{3,2,1,0:T(8,128)}, f32[2,2,128,512]{3,2,1,0:T(8,128)S(1)}, u32[]{:S(2)}, u32[]{:S(2)}) collective-permute-start(f32[2,2,128,512]{3,2,1,0:T(8,128)} %get-tuple-element.25.refs_3_.stiff), channel_id=1, source_target_pairs={{0,1},{1,0},{2,3},{3,2},{4,5},{5,4},{6,7},{7,6},{8,9},{9,8},{10,11... | collective-permute-start | bytes 3145736 | tf_op jit(solution)/shard_map/ppermute | solution.py:791
  34.2 2.6 collective-permute-start.5
  34.2 93.3 %collective-permute-start.3 = (f32[1,16,128,512]{3,2,1,0:T(8,128)}, f32[1,16,128,512]{3,2,1,0:T(8,128)}, u32[]{:S(2)}, u32[]{:S(2)}) collective-permute-start(f32[1,16,128,512]{3,2,1,0:T(8,128)} %get-tuple-element.24), channel_id=1, source_target_pairs={{0,16},{16,0},{1,17},{17,1},{2,18},{18,2},{3,19},{19,3},{4,20},{20... | collective-permute-start | bytes 12582920 | tf_op jit(solution)/shard_map/ppermute | solution.py:794
  42.6 24.2 %all-to-all-start = ((f32[8,2,3,32,128]{4,3,2,1,0:T(8,128)}), f32[8,2,3,32,128]{4,3,2,1,0:T(8,128)S(1)}, u32[]{:S(2)}, u32[]{:S(2)}) async-start(f32[8,2,3,32,128]{4,3,2,1,0:T(8,128)} %forward_columns.4), calls=%async_computation | async-start | bytes 1572864 | tf_op jit(solution)/shard_map/all_to_all | solution.py:830
  46.9 20.0 %copy-start.10 = (bf16[512,512]{1,0:T(8,128)(2,1)S(1)}, bf16[512,512]{1,0:T(8,128)(2,1)}, u32[]{:S(2)}) copy-start(bf16[512,512]{1,0:T(8,128)(2,1)} %constant.43.clone.refs_4_) | copy-start | bytes 1572868
  46.9 20.0 %copy-start.11 = (bf16[512,512]{1,0:T(8,128)(2,1)S(1)}, bf16[512,512]{1,0:T(8,128)(2,1)}, u32[]{:S(2)}) copy-start(bf16[512,512]{1,0:T(8,128)(2,1)} %constant.42.clone.refs_3_) | copy-start | bytes 1572868
  46.9 20.0 %copy-start.19 = (f32[8,256]{1,0:T(8,128)S(1)}, f32[8,256]{1,0:T(8,128)}, u32[]{:S(2)}) copy-start(f32[8,256]{1,0:T(8,128)} %constant.41.clone.refs_2_) | copy-start | bytes 24580
  46.9 20.0 %copy-start.22 = (s32[5]{0:T(128)S(1)}, s32[5]{0:T(128)}, u32[]{:S(2)}) copy-start(s32[5]{0:T(128)} %get-tuple-element.42.refs_0_.places) | copy-start | bytes 64
  57.8 37.3 %copy-start = (bf16[1,512,512]{2,1,0:T(8,128)(2,1)S(1)}, bf16[1,512,512]{2,1,0:T(8,128)(2,1)}, u32[]{:S(2)}) copy-start(bf16[1,512,512]{2,1,0:T(8,128)(2,1)} %get-tuple-element.38.refs_16_.refs_8_.low.refs_10_) | copy-start | bytes 1572868
  57.8 37.3 %copy-start.3 = (bf16[1,512,512]{2,1,0:T(8,128)(2,1)S(1)}, bf16[1,512,512]{2,1,0:T(8,128)(2,1)}, u32[]{:S(2)}) copy-start(bf16[1,512,512]{2,1,0:T(8,128)(2,1)} %get-tuple-element.39.refs_15_.refs_7_.high.refs_9_) | copy-start | bytes 1572868
  96.0 2.4 collective-permute-start.6
  136.9 35.9 %copy-start.46 = (f32[1,16,512]{2,1,0:T(8,128)S(1)}, f32[1,16,512]{2,1,0:T(8,128)}, u32[]{:S(2)}) copy-start(f32[1,16,512]{2,1,0:T(8,128)} %get-tuple-element.33) | copy-start | bytes 98308
  136.9 37.9 %copy-start.45 = (f32[1,16,512]{2,1,0:T(8,128)S(1)}, f32[1,16,512]{2,1,0:T(8,128)}, u32[]{:S(2)}) copy-start(f32[1,16,512]{2,1,0:T(8,128)} %get-tuple-element.34) | copy-start | bytes 98308
  136.9 40.9 %copy-start.42 = (f32[1,128,32]{2,1,0:T(8,128)S(1)}, f32[1,128,32]{2,1,0:T(8,128)}, u32[]{:S(2)}) copy-start(f32[1,128,32]{2,1,0:T(8,128)} %get-tuple-element.35) | copy-start | bytes 49156
  136.9 2.6 collective-permute-start.11
  169.2 39.2 %all-to-all-start.5 = ((f32[8,2,3,32,128]{4,3,2,1,0:T(8,128)}), f32[8,2,3,32,128]{4,3,2,1,0:T(8,128)S(1)}, u32[]{:S(2)}, u32[]{:S(2)}) async-start(f32[8,2,3,32,128]{4,3,2,1,0:T(8,128)} %forward_columns.5.refs_5_), calls=%async_computation.5 | async-start | bytes 1572864 | tf_op jit(solution)/shard_map/all_to_all | solution.py:830
  172.8 18.6 %collective-permute-start.12 = (f32[1,16,512]{2,1,0:T(8,128)S(1)}, f32[1,16,512]{2,1,0:T(8,128)S(1)}, u32[]{:S(2)}, u32[]{:S(2)}) collective-permute-start(f32[1,16,512]{2,1,0:T(8,128)S(1)} %copy-done.46), channel_id=1, source_target_pairs={{0,2},{2,4},{4,6},{6,8},{8,10},{10,12},{12,14},{14,0},{1,3},{3,5},... | collective-permute-start | bytes 98312 | tf_op jit(solution)/shard_map/ppermute | solution.py:809
  174.8 16.6 %collective-permute-start.13 = (f32[1,16,512]{2,1,0:T(8,128)S(1)}, f32[1,16,512]{2,1,0:T(8,128)S(1)}, u32[]{:S(2)}, u32[]{:S(2)}) collective-permute-start(f32[1,16,512]{2,1,0:T(8,128)S(1)} %copy-done.45), channel_id=1, source_target_pairs={{2,0},{4,2},{6,4},{8,6},{10,8},{12,10},{14,12},{0,14},{3,1},{5,3},... | collective-permute-start | bytes 98312 | tf_op jit(solution)/shard_map/ppermute | solution.py:810
  177.8 1.3 collective-permute-start.14
  179.0 12.4 %copy-start.35 = (f32[1,128,32]{2,1,0:T(8,128)}, f32[1,128,32]{2,1,0:T(8,128)S(1)}, u32[]{:S(2)}) copy-start(f32[1,128,32]{2,1,0:T(8,128)S(1)} %collective-permute-done.14.refs_10_) | copy-start | bytes 49156
  192.0 10.9 %copy-start.20 = (s32[5]{0:T(128)S(1)}, s32[5]{0:T(128)}, u32[]{:S(2)}) copy-start(s32[5]{0:T(128)} %get-tuple-element.43.refs_0_.places) | copy-start | bytes 64
  205.1 10.3 %copy-start.23 = (s32[5]{0:T(128)S(1)}, s32[5]{0:T(128)}, u32[]{:S(2)}) copy-start(s32[5]{0:T(128)} %get-tuple-element.42.refs_0_.places) | copy-start | bytes 64
  208.3 30.5 %copy-start.1 = (bf16[1,512,512]{2,1,0:T(8,128)(2,1)S(1)}, bf16[1,512,512]{2,1,0:T(8,128)(2,1)}, u32[]{:S(2)}) copy-start(bf16[1,512,512]{2,1,0:T(8,128)(2,1)} %get-tuple-element.38.refs_16_.refs_8_.low.refs_10_) | copy-start | bytes 1572868
  208.3 30.5 %copy-start.4 = (bf16[1,512,512]{2,1,0:T(8,128)(2,1)S(1)}, bf16[1,512,512]{2,1,0:T(8,128)(2,1)}, u32[]{:S(2)}) copy-start(bf16[1,512,512]{2,1,0:T(8,128)(2,1)} %get-tuple-element.39.refs_15_.refs_7_.high.refs_9_) | copy-start | bytes 1572868
  208.3 26.3 %all-to-all-start.3 = ((f32[8,2,3,32,128]{4,3,2,1,0:T(8,128)}), f32[8,2,3,32,128]{4,3,2,1,0:T(8,128)}, u32[]{:S(2)}, u32[]{:S(2)}) async-start(f32[8,2,3,32,128]{4,3,2,1,0:T(8,128)} %copy-done.18), calls=%async_computation.3 | async-start | bytes 1572864 | tf_op jit(solution)/shard_map/all_to_all | solution.py:830
  213.6 99.2 %collective-permute-start.7 = (f32[1,16,128,512]{3,2,1,0:T(8,128)}, f32[1,16,128,512]{3,2,1,0:T(8,128)}, u32[]{:S(2)}, u32[]{:S(2)}) collective-permute-start(f32[1,16,128,512]{3,2,1,0:T(8,128)} %get-tuple-element.27.refs_1_.refs_2_.refs_3_.refs_4_.phi), channel_id=1, source_target_pairs={{0,16},{16,0},{1,17},{17,1},{2,18},{18,2},{3,19},{19,3},{4,20},{20... | collective-permute-start | bytes 12582920 | tf_op jit(solution)/shard_map/ppermute | solution.py:794
  234.6 24.2 %all-to-all-start.6 = ((f32[8,2,3,32,128]{4,3,2,1,0:T(8,128)}), f32[8,2,3,32,128]{4,3,2,1,0:T(8,128)}, u32[]{:S(2)}, u32[]{:S(2)}) async-start(f32[8,2,3,32,128]{4,3,2,1,0:T(8,128)} %copy-done.17), calls=%async_computation.6 | async-start | bytes 1572864 | tf_op jit(solution)/shard_map/all_to_all | solution.py:830
  240.8 2.4 copy-start.12
  240.8 21.5 %copy-start.2 = (bf16[1,512,512]{2,1,0:T(8,128)(2,1)S(1)}, bf16[1,512,512]{2,1,0:T(8,128)(2,1)}, u32[]{:S(2)}) copy-start(bf16[1,512,512]{2,1,0:T(8,128)(2,1)} %get-tuple-element.38.refs_16_.refs_8_.low.refs_10_) | copy-start | bytes 1572868
  240.8 21.5 %copy-start.5 = (bf16[1,512,512]{2,1,0:T(8,128)(2,1)S(1)}, bf16[1,512,512]{2,1,0:T(8,128)(2,1)}, u32[]{:S(2)}) copy-start(bf16[1,512,512]{2,1,0:T(8,128)(2,1)} %get-tuple-element.39.refs_15_.refs_7_.high.refs_9_) | copy-start | bytes 1572868
  240.8 2.4 collective-permute-start.15
  258.8 23.9 %all-to-all-start.4 = ((f32[8,2,3,32,128]{4,3,2,1,0:T(8,128)}), f32[8,2,3,32,128]{4,3,2,1,0:T(8,128)S(1)}, u32[]{:S(2)}, u32[]{:S(2)}) async-start(f32[8,2,3,32,128]{4,3,2,1,0:T(8,128)} %forward_columns.7), calls=%async_computation.4 | async-start | bytes 1572864 | tf_op jit(solution)/shard_map/all_to_all | solution.py:830
  264.3 18.3 %copy-start.21 = (s32[5]{0:T(128)S(1)}, s32[5]{0:T(128)}, u32[]{:S(2)}) copy-start(s32[5]{0:T(128)} %get-tuple-element.43.refs_0_.places) | copy-start | bytes 64
  264.3 2.4 collective-permute-start.16
  282.6 3.4 copy-start.9
  287.4 6.8 %copy-start.44 = (f32[1,16,512]{2,1,0:T(8,128)S(1)}, f32[1,16,512]{2,1,0:T(8,128)}, u32[]{:S(2)}) copy-start(f32[1,16,512]{2,1,0:T(8,128)} %get-tuple-element.29) | copy-start | bytes 98308
  287.4 8.8 %copy-start.43 = (f32[1,16,512]{2,1,0:T(8,128)S(1)}, f32[1,16,512]{2,1,0:T(8,128)}, u32[]{:S(2)}) copy-start(f32[1,16,512]{2,1,0:T(8,128)} %get-tuple-element.30) | copy-start | bytes 98308
  287.4 11.6 %copy-start.41 = (f32[1,128,32]{2,1,0:T(8,128)S(1)}, f32[1,128,32]{2,1,0:T(8,128)}, u32[]{:S(2)}) copy-start(f32[1,128,32]{2,1,0:T(8,128)} %get-tuple-element.31) | copy-start | bytes 49156
  290.6 34.5 %all-to-all-start.7 = ((f32[8,2,3,32,128]{4,3,2,1,0:T(8,128)}), f32[8,2,3,32,128]{4,3,2,1,0:T(8,128)S(1)}, u32[]{:S(2)}, u32[]{:S(2)}) async-start(f32[8,2,3,32,128]{4,3,2,1,0:T(8,128)} %row_lines.7), calls=%async_computation.7 | async-start | bytes 1572864 | tf_op jit(solution)/shard_map/all_to_all | solution.py:830
  294.2 18.6 %collective-permute-start.8 = (f32[1,16,512]{2,1,0:T(8,128)S(1)}, f32[1,16,512]{2,1,0:T(8,128)S(1)}, u32[]{:S(2)}, u32[]{:S(2)}) collective-permute-start(f32[1,16,512]{2,1,0:T(8,128)S(1)} %copy-done.44), channel_id=1, source_target_pairs={{0,2},{2,4},{4,6},{6,8},{8,10},{10,12},{12,14},{14,0},{1,3},{3,5},... | collective-permute-start | bytes 98312 | tf_op jit(solution)/shard_map/ppermute | solution.py:809
  296.2 16.6 %collective-permute-start.9 = (f32[1,16,512]{2,1,0:T(8,128)S(1)}, f32[1,16,512]{2,1,0:T(8,128)S(1)}, u32[]{:S(2)}, u32[]{:S(2)}) collective-permute-start(f32[1,16,512]{2,1,0:T(8,128)S(1)} %copy-done.43), channel_id=1, source_target_pairs={{2,0},{4,2},{6,4},{8,6},{10,8},{12,10},{14,12},{0,14},{3,1},{5,3},... | collective-permute-start | bytes 98312 | tf_op jit(solution)/shard_map/ppermute | solution.py:810
  299.0 1.3 collective-permute-start.10
  300.2 12.6 %copy-start.34 = (f32[1,128,32]{2,1,0:T(8,128)}, f32[1,128,32]{2,1,0:T(8,128)S(1)}, u32[]{:S(2)}) copy-start(f32[1,128,32]{2,1,0:T(8,128)S(1)} %collective-permute-done.10.refs_11_) | copy-start | bytes 49156
  328.1 2.4 collective-permute-start.17
  (23 other events, 28.1 us)
